TPU v7x, 128 devices: a whole 4x4x4 slice. The times are simulated.
128 devices in a mesh: ty: 8 (over x, core), tx: 16 (over z, y).
Axes of the slice: x: 4, y: 4, z: 4, core: 2. Of those that a mesh axis runs over, the one named last changes fastest.
Arguments:
- spectrum: float32 [2, 4096, 8192], P(None, 'ty', 'tx')
- measured: float32 [128, 256, 256], P(('ty', 'tx')), may hold values from 0.5 to 6
- pupil_mask: int32 [256, 256], replicated, may hold values 0 or 1
- led_count: int32 [128], replicated, may hold values from 4 to 8, as said below
- led_owner: int32 [128, 8], replicated, may hold values from 0 to 15, as said below
- led_offset: int32 [128, 8, 2], replicated, may hold values from 0 to 256
Outputs:
- spectrum_step: float32 [2, 4096, 8192], P(None, 'ty', 'tx')
- cg_residual: float32 [2, 4096, 8192], P(None, 'ty', 'tx')
Inputs may be any that keep to these rules, and one draw needn't show every extreme that they name: Capture c lights the LEDs of slots 0 to led_count[c] - 1; some capture lights 8 in every draw. `led_owner`: for capture c, taken on device (c // 16, c % 16) of the mesh (ty, tx), slot t names the column of the tile in tile row c // 16 that holds the slot's block. The live slots of one capture name distinct tiles. No tile holds the blocks of more than 8 live slots over the captures of its tile row, and in every tile row some tile holds exactly 8. `led_offset`: every block lies inside the tile named by led_owner.
All inputs are finite; a program needn't handle non-finite values.
Results may differ from a plain program's by a relative error of at most 0.0003.
Values sent between devices are 32-bit elements; how exact they have to be, the bound alone decides.
A program may use at most 128 MiB of HBM per device.

v0:
```python
import jax
import jax.numpy as jnp
from jax import lax
from jax.sharding import PartitionSpec as P

ITERS = 2


REG = 0.5


def extended(array, sides, width):
    for axis, dim in sides:
        size, length = (lax.axis_size(axis), array.shape[dim])
        up = [(i, (i + 1) % size) for i in range(size - 1)]
        down = [(j, i) for i, j in up]
        last = lax.slice_in_dim(array, length - width, length, axis=dim)
        initial = lax.slice_in_dim(array, 0, width, axis=dim)
        before = lax.ppermute(last, axis, up)
        after = lax.ppermute(initial, axis, down)
        array = jnp.concatenate([before, array, after], axis=dim)
    return array


def dft_tables(side_len):
    indices = jnp.arange(side_len, dtype=jnp.int32)
    product = indices[:, None] * indices[None, :] % side_len
    angles = product.astype(jnp.float32) * (2.0 * jnp.pi / side_len)
    scale_one = 1.0 / jnp.sqrt(jnp.asarray(side_len, jnp.float32))
    return (jnp.cos(angles) * scale_one, jnp.sin(angles) * scale_one)


def transform(real_part, imag_part, cosine_table, sine_table, orient):
    highest = lax.Precision.HIGHEST
    left_real = jnp.einsum(
        "jk,skl->sjl", cosine_table, real_part, precision=highest
    ) - orient * jnp.einsum("jk,skl->sjl", sine_table, imag_part, precision=highest)
    left_imag = jnp.einsum(
        "jk,skl->sjl", cosine_table, imag_part, precision=highest
    ) + orient * jnp.einsum("jk,skl->sjl", sine_table, real_part, precision=highest)
    out_real = jnp.einsum(
        "sjk,kl->sjl", left_real, cosine_table, precision=highest
    ) - orient * jnp.einsum("sjk,kl->sjl", left_imag, sine_table, precision=highest)
    out_imag = jnp.einsum(
        "sjk,kl->sjl", left_imag, cosine_table, precision=highest
    ) + orient * jnp.einsum("sjk,kl->sjl", left_real, sine_table, precision=highest)
    return (out_real, out_imag)


def laplace(values):
    padded = extended(values, (("ty", 1), ("tx", 2)), 1)
    neighbours = (
        padded[:, 2:, 1:-1] + padded[:, :-2, 1:-1] + padded[:, 1:-1, 2:] + padded[:, 1:-1, :-2]
    )
    return 4.0 * values - neighbours


def squared(values):
    return lax.psum(jnp.sum(values * values), ("ty", "tx"))


def on_device(spectrum, measured, pupil_mask, led_count, led_owner, led_offset):
    highest = lax.Precision.HIGHEST
    block_side = pupil_mask.shape[0]
    slot_count = led_owner.shape[1]
    cosine_table, sine_table = dft_tables(block_side)
    pupil = pupil_mask.astype(jnp.float32)
    across = lax.axis_size("tx")
    row_start = lax.axis_index("ty") * across
    column = lax.axis_index("tx")
    row_owner = lax.dynamic_slice_in_dim(led_owner, row_start, across, 0)
    row_count = lax.dynamic_slice_in_dim(led_count, row_start, across, 0)
    row_offset = lax.dynamic_slice_in_dim(led_offset, row_start, across, 0)
    slot_ids = jnp.arange(slot_count, dtype=jnp.int32)
    live_slots = slot_ids[None, :] < row_count[:, None]
    matched = ((row_owner == column) & live_slots).astype(jnp.int32)
    served = jnp.sum(matched, axis=1)
    corner_by_dest = jnp.sum(matched[:, :, None] * row_offset, axis=1)
    rank_of = jnp.cumsum(served) - served
    chosen = served[None, :] * (rank_of[None, :] == slot_ids[:, None]).astype(jnp.int32)
    corners = jnp.sum(chosen[:, :, None] * corner_by_dest[None, :, :], axis=1)
    active = jnp.sum(chosen, axis=1).astype(jnp.float32)[:, None, None]
    selector = chosen.astype(jnp.float32)
    own_owner = lax.dynamic_slice_in_dim(row_owner, column, 1, 0)[0]
    own_live = lax.dynamic_slice_in_dim(live_slots, column, 1, 0)[0]
    tile_ids = jnp.arange(across, dtype=jnp.int32)
    needed = jnp.sum(
        ((own_owner[:, None] == tile_ids[None, :]) & own_live[:, None]).astype(jnp.float32), axis=0
    )
    anchor = jnp.zeros((), jnp.int32)

    def extract(values):
        blocks = jnp.stack(
            [
                lax.dynamic_slice(
                    values,
                    (anchor, corners[slot_no, 0], corners[slot_no, 1]),
                    (2, block_side, block_side),
                )
                for slot_no in range(slot_count)
            ]
        )
        return (blocks[:, 0] * pupil, blocks[:, 1] * pupil)

    field_real, field_imag = transform(*extract(spectrum), cosine_table, sine_table, 1.0)

    def to_capture(images):
        dest_term = jnp.einsum("sd,sij->dij", selector, images, precision=highest)
        arrived = lax.all_to_all(dest_term, "tx", split_axis=0, concat_axis=0, tiled=True)
        return jnp.sum(arrived, axis=0)

    def to_owners(capture_img):
        copies = capture_img[None] * needed[:, None, None]
        arrived = lax.all_to_all(copies, "tx", split_axis=0, concat_axis=0, tiled=True)
        return jnp.einsum("sd,dij->sij", selector, arrived, precision=highest)

    def adjoint(capture_img):
        returned = to_owners(capture_img)
        back_real, back_imag = transform(
            2.0 * field_real * returned, 2.0 * field_imag * returned, cosine_table, sine_table, -1.0
        )
        contrib = jnp.stack([back_real * pupil * active, back_imag * pupil * active], axis=1)
        deposit = jnp.zeros_like(spectrum)
        for slot_no in range(slot_count):
            corner = (anchor, corners[slot_no, 0], corners[slot_no, 1])
            window = lax.dynamic_slice(deposit, corner, (2, block_side, block_side))
            deposit = lax.dynamic_update_slice(deposit, window + contrib[slot_no], corner)
        return deposit

    intensity = to_capture((field_real * field_real + field_imag * field_imag) * active)
    misfit = intensity - measured[0]
    gradient = adjoint(misfit) + REG * laplace(spectrum)
    spectrum_step = jnp.zeros_like(spectrum)
    cg_residual = -gradient
    heading = cg_residual
    res_norm = squared(cg_residual)
    for round_no in range(ITERS):
        lin_real, lin_imag = transform(*extract(heading), cosine_table, sine_table, 1.0)
        applied = adjoint(
            to_capture(2.0 * (field_real * lin_real + field_imag * lin_imag) * active)
        ) + REG * laplace(heading)
        step_len = res_norm / lax.psum(jnp.sum(heading * applied), ("ty", "tx"))
        spectrum_step = spectrum_step + step_len * heading
        cg_residual = cg_residual - step_len * applied
        new_norm = squared(cg_residual)
        heading = cg_residual + new_norm / res_norm * heading
        res_norm = new_norm
    return (spectrum_step, cg_residual)


def solution(mesh):
    placed = (P(None, "ty", "tx"), P(("ty", "tx"), None, None), P(), P(), P(), P())
    return jax.shard_map(
        on_device,
        mesh=mesh,
        in_specs=placed,
        out_specs=(P(None, "ty", "tx"), P(None, "ty", "tx")),
        check_vma=False,
    )
```

profile of v0, /device:TPU:1, one launch (start us, length us, event | category | flops | bytes accessed | tf_op | source)
XLA Modules:
  0.0 1147.6 jit_solution(6498343180733534252)
XLA Ops:
  71.4 6.5 add_multiply_fusion.2
  86.6 8.8 all-to-all-start
  95.9 62.0 %all-to-all-done = f32[16,256,256]{2,1,0:T(8,128)} async-done(((f32[16,256,256]{2,1,0:T(8,128)}), f32[16,256,256]{2,1,0:T(8,128)}, u32[]{:S(2)}, u32[]{:S(2)}) %all-to-all-start) | async-done | bytes 4194336 | tf_op jit(solution)/shard_map/all_to_all | solution.py:109
  183.1 41.0 %collective-permute-done.2 = f32[2,514,1]{1,0,2:T(2,128)S(1)} collective-permute-done((f32[2,514,1]{1,0,2:T(2,128)S(1)}, f32[2,514,1]{1,0,2:T(2,128)S(1)}, u32[]{:S(2)}, u32[]{:S(2)}) %collective-permute-start.2) | collective-permute-done | bytes 4144 | tf_op jit(solution)/shard_map/ppermute | solution.py:20
  227.0 7.0 fusion.4
  302.3 6.5 dynamic_update_slice.75
  311.1 6.5 dynamic_update_slice.76
  342.4 8.4 fusion.585
  396.1 53.3 %all_to_all.30 = f32[16,256,256]{2,1,0:T(8,128)} all-to-all(f32[16,256,256]{2,1,0:T(8,128)S(1)} %copy.333), channel_id=1, replica_groups=mesh['ty'=8,'tx'=16] {'tx'}, dimensions={0} | all-to-all | bytes 8388608 | tf_op jit(solution)/shard_map/all_to_all | solution.py:109
  476.8 33.1 %collective-permute-done.6 = f32[2,514,1]{1,0,2:T(2,128)S(1)} collective-permute-done((f32[2,514,1]{1,0,2:T(2,128)S(1)}, f32[2,514,1]{1,0,2:T(2,128)S(1)}, u32[]{:S(2)}, u32[]{:S(2)}) %collective-permute-start.6) | collective-permute-done | bytes 4144 | tf_op jit(solution)/shard_map/ppermute | solution.py:20
  513.3 7.0 fusion.2
  571.2 6.5 dynamic_update_slice.81
  588.6 6.5 dynamic_update_slice.83
  597.5 6.5 dynamic_update_slice.84
  629.0 10.3 multiply_reduce_fusion.2
  639.3 72.9 %all-reduce = (f32[]{:T(128)}, f32[]{:T(128)}) all-reduce(f32[]{:T(128)} %get-tuple-element.3, f32[]{:T(128)} %get-tuple-element.2), channel_id=1, replica_groups=mesh['ty'=8,'tx'=16] {'ty','tx'}, use_global_device_ids=true, to_apply=%region_8.9 | all-reduce | flops 2 | bytes 16 | tf_op jit(solution)/shard_map/psum | solution.py:59
  716.9 62.7 %psum.30 = f32[]{:T(128)} all-reduce(f32[]{:T(128)} %multiply_reduce_fusion.1), channel_id=1, replica_groups=mesh['ty'=8,'tx'=16] {'ty','tx'}, use_global_device_ids=true, to_apply=%region_13.14 | all-reduce | flops 1 | bytes 8 | tf_op jit(solution)/shard_map/psum | solution.py:59
  829.0 53.9 %all_to_all.31 = f32[16,256,256]{2,1,0:T(8,128)} all-to-all(f32[16,256,256]{2,1,0:T(8,128)S(1)} %copy.359), channel_id=1, replica_groups=mesh['ty'=8,'tx'=16] {'tx'}, dimensions={0} | all-to-all | bytes 8388608 | tf_op jit(solution)/shard_map/all_to_all | solution.py:109
  907.6 41.3 %collective-permute-done.10 = f32[2,514,1]{1,0,2:T(2,128)S(1)} collective-permute-done((f32[2,514,1]{1,0,2:T(2,128)S(1)}, f32[2,514,1]{1,0,2:T(2,128)S(1)}, u32[]{:S(2)}, u32[]{:S(2)}) %collective-permute-start.10) | collective-permute-done | bytes 4144 | tf_op jit(solution)/shard_map/ppermute | solution.py:20
  951.9 7.0 fusion
  1026.7 6.5 dynamic_update_slice.91
  1035.5 6.5 dynamic_update_slice.92
  1066.5 8.6 multiply_reduce_fusion
  1075.1 65.3 %psum.31 = f32[]{:T(128)} all-reduce(f32[]{:T(128)} %multiply_reduce_fusion), channel_id=1, replica_groups=mesh['ty'=8,'tx'=16] {'ty','tx'}, use_global_device_ids=true, to_apply=%region_16.17 | all-reduce | flops 1 | bytes 8 | tf_op jit(solution)/shard_map/psum | solution.py:142
  (225 shorter events, 517.1 us)
Async XLA Ops:
  0.6 37.5 %copy-start.13 = (f32[2,512,512]{2,1,0:T(8,128)S(1)}, f32[2,512,512]{2,1,0:T(8,128)}, u32[]{:S(2)}) copy-start(f32[2,512,512]{2,1,0:T(8,128)} %param.6) | copy-start | bytes 6291460
  86.6 9.0 copy-start.15
  86.6 71.2 %all-to-all-start = ((f32[16,256,256]{2,1,0:T(8,128)}), f32[16,256,256]{2,1,0:T(8,128)}, u32[]{:S(2)}, u32[]{:S(2)}) async-start(f32[16,256,256]{2,1,0:T(8,128)} %copy.306), calls=%async_computation | async-start | bytes 8388608 | tf_op jit(solution)/shard_map/all_to_all | solution.py:109
  95.9 64.5 %copy-start.14 = (f32[1,256,256]{2,1,0:T(8,128)S(1)}, f32[1,256,256]{2,1,0:T(8,128)}, u32[]{:S(2)}) copy-start(f32[1,256,256]{2,1,0:T(8,128)} %param.7) | copy-start | bytes 786436
  162.8 64.2 %all-to-all-start.1 = ((f32[16,256,256]{2,1,0:T(8,128)}), f32[16,256,256]{2,1,0:T(8,128)}, u32[]{:S(2)}, u32[]{:S(2)}) async-start(f32[16,256,256]{2,1,0:T(8,128)} %broadcast_multiply_fusion.2), calls=%async_computation.1 | async-start | bytes 8388608 | tf_op jit(solution)/shard_map/all_to_all | solution.py:114
  168.1 6.9 collective-permute-start
  172.0 3.8 collective-permute-start.1
  177.4 46.7 %collective-permute-start.2 = (f32[2,514,1]{1,0,2:T(2,128)S(1)}, f32[2,514,1]{1,0,2:T(2,128)S(1)}, u32[]{:S(2)}, u32[]{:S(2)}) collective-permute-start(f32[2,514,1]{1,0,2:T(2,128)S(1)} %copy.320), channel_id=1, source_target_pairs={{1,0},{2,1},{3,2},{4,3},{5,4},{6,5},{7,6},{8,7},{9,8},{10,9},{11,1... | collective-permute-start | bytes 12344 | tf_op jit(solution)/shard_map/ppermute | solution.py:20
  179.0 45.4 %collective-permute-start.3 = (f32[2,514,1]{1,0,2:T(2,128)S(1)}, f32[2,514,1]{1,0,2:T(2,128)S(1)}, u32[]{:S(2)}, u32[]{:S(2)}) collective-permute-start(f32[2,514,1]{1,0,2:T(2,128)S(1)} %copy.322), channel_id=1, source_target_pairs={{0,1},{1,2},{2,3},{3,4},{4,5},{5,6},{6,7},{7,8},{8,9},{9,10},{10,1... | collective-permute-start | bytes 12344 | tf_op jit(solution)/shard_map/ppermute | solution.py:19
  234.1 4.8 copy-start.5
  268.0 5.2 copy-start.1
  454.4 58.9 %all-to-all-start.3 = ((f32[16,256,256]{2,1,0:T(8,128)}), f32[16,256,256]{2,1,0:T(8,128)}, u32[]{:S(2)}, u32[]{:S(2)}) async-start(f32[16,256,256]{2,1,0:T(8,128)} %broadcast_multiply_fusion.1), calls=%async_computation.3 | async-start | bytes 8388608 | tf_op jit(solution)/shard_map/all_to_all | solution.py:114
  459.7 9.1 collective-permute-start.4
  465.2 4.4 collective-permute-start.5
  471.3 38.7 %collective-permute-start.6 = (f32[2,514,1]{1,0,2:T(2,128)S(1)}, f32[2,514,1]{1,0,2:T(2,128)S(1)}, u32[]{:S(2)}, u32[]{:S(2)}) collective-permute-start(f32[2,514,1]{1,0,2:T(2,128)S(1)} %copy.346), channel_id=1, source_target_pairs={{1,0},{2,1},{3,2},{4,3},{5,4},{6,5},{7,6},{8,7},{9,8},{10,9},{11,1... | collective-permute-start | bytes 12344 | tf_op jit(solution)/shard_map/ppermute | solution.py:20
  472.8 37.4 %collective-permute-start.7 = (f32[2,514,1]{1,0,2:T(2,128)S(1)}, f32[2,514,1]{1,0,2:T(2,128)S(1)}, u32[]{:S(2)}, u32[]{:S(2)}) collective-permute-start(f32[2,514,1]{1,0,2:T(2,128)S(1)} %copy.348), channel_id=1, source_target_pairs={{0,1},{1,2},{2,3},{3,4},{4,5},{5,6},{6,7},{7,8},{8,9},{9,10},{10,1... | collective-permute-start | bytes 12344 | tf_op jit(solution)/shard_map/ppermute | solution.py:19
  520.3 4.8 copy-start.7
  554.2 5.2 copy-start.2
  887.8 64.1 %all-to-all-start.5 = ((f32[16,256,256]{2,1,0:T(8,128)}), f32[16,256,256]{2,1,0:T(8,128)}, u32[]{:S(2)}, u32[]{:S(2)}) async-start(f32[16,256,256]{2,1,0:T(8,128)} %broadcast_multiply_fusion), calls=%async_computation.5 | async-start | bytes 8388608 | tf_op jit(solution)/shard_map/all_to_all | solution.py:114
  893.2 6.5 collective-permute-start.8
  897.2 3.2 collective-permute-start.9
  902.1 46.8 %collective-permute-start.10 = (f32[2,514,1]{1,0,2:T(2,128)S(1)}, f32[2,514,1]{1,0,2:T(2,128)S(1)}, u32[]{:S(2)}, u32[]{:S(2)}) collective-permute-start(f32[2,514,1]{1,0,2:T(2,128)S(1)} %copy.378), channel_id=1, source_target_pairs={{1,0},{2,1},{3,2},{4,3},{5,4},{6,5},{7,6},{8,7},{9,8},{10,9},{11,1... | collective-permute-start | bytes 12344 | tf_op jit(solution)/shard_map/ppermute | solution.py:20
  903.6 45.6 %collective-permute-start.11 = (f32[2,514,1]{1,0,2:T(2,128)S(1)}, f32[2,514,1]{1,0,2:T(2,128)S(1)}, u32[]{:S(2)}, u32[]{:S(2)}) collective-permute-start(f32[2,514,1]{1,0,2:T(2,128)S(1)} %copy.380), channel_id=1, source_target_pairs={{0,1},{1,2},{2,3},{3,4},{4,5},{5,6},{6,7},{7,8},{8,9},{9,10},{10,1... | collective-permute-start | bytes 12344 | tf_op jit(solution)/shard_map/ppermute | solution.py:19
  1066.5 75.2 %copy-start.11 = (f32[2,512,512]{2,1,0:T(8,128)S(1)}, f32[2,512,512]{2,1,0:T(8,128)}, u32[]{:S(2)}) copy-start(f32[2,512,512]{2,1,0:T(8,128)} %copy-done.10) | copy-start | bytes 6291460
  (8 other events, 21.1 us)
where the time goes:
time: 1160 us; the launch traced here: 1150 us
  blocking collectives  308 us (27%)
  matrix products  263 us (23%)
  waiting for transfers between devices  187 us (16%)
  local copies, waits for them, and re-layouts  180 us (16%)
  other arithmetic  112 us (10%)
  starting transfers between devices  60.8 us (5%)
  between operations  35.9 us (3%)
    dynamic_update_slice x24, local copies, waits for them, and re-layouts, adjoint(): lax.dynamic_update_slice(deposit, window + contrib[slot_no], corner)  150 us
    psum x2, blocking collectives, squared(): return lax.psum(jnp.sum(values * values), ('ty', 'tx'))  136 us
    ppermute x6, waiting for transfers between devices, extended(): after = lax.ppermute(initial, axis, down)  115 us
    all_to_all x2, blocking collectives, to_capture(): lax.all_to_all(dest_term, 'tx', split_axis=0, concat_axis=0, tiled=True)  107 us
    psum x1, blocking collectives, on_device(): step_len = res_norm / lax.psum(jnp.sum(heading * applied), ('ty', 'tx'))  65.3 us
    all_to_all x1, waiting for transfers between devices, to_capture(): lax.all_to_all(dest_term, 'tx', split_axis=0, concat_axis=0, tiled=True)  62 us
    add x21, other arithmetic, adjoint(): window + contrib[slot_no]  48.2 us
    dot_general x6, matrix products, transform(): jnp.einsum('sjk,kl->sjl', left_real, cosine_table, precision=highest)  30.1 us
  transfers between devices with their start and end apart: 16, of which 10 were waited for; matrix products, arithmetic and copies ran while one was open for 1% of the time, Pallas kernels for 0%

commit v1 on v0

v1 whole, which is shorter than its diff:
```python
import jax
import jax.numpy as jnp
import numpy as np
from jax import lax
from jax.experimental import pallas as pl
from jax.experimental.pallas import tpu as pltpu
from jax.sharding import PartitionSpec as P

B = 256
H = 128
T = 512
S = 8
N = 16
REG = 0.5
F32 = jnp.float32
BF = jnp.bfloat16
MESH = pl.DeviceIdType.MESH
VM = pl.BlockSpec(memory_space=pltpu.VMEM)
SM = pl.BlockSpec(memory_space=pltpu.SMEM)


def tables():
    m = np.arange(H)
    out = []
    for p in range(2):
        ang = ((2 * m[:, None] + p) * m[None, :] % B) * (2.0 * np.pi / B)
        re, im = np.cos(ang) / 16.0, np.sin(ang) / 16.0
        out.append(np.block([[re, -im], [im, re]]))
    full = np.stack([out[0], out[1], out[0].T, out[1].T])
    hi = full.astype(np.float32).astype(jnp.bfloat16)
    lo = (full - hi.astype(np.float64)).astype(np.float32).astype(jnp.bfloat16)
    return jnp.asarray(np.stack([hi, lo]))


def split(x):
    hi = x.astype(BF)
    return hi, (x - hi.astype(F32)).astype(BF)


def mm(a, b):
    return jnp.dot(a, b, preferred_element_type=F32)


def left(tab, k, x):
    hi, lo = split(x)
    return mm(tab[0, k], hi) + (mm(tab[0, k], lo) + mm(tab[1, k], hi))


def right(tab, k, x):
    hi, lo = split(x)
    return mm(hi, tab[0, k]) + (mm(lo, tab[0, k]) + mm(hi, tab[1, k]))


def masks(r, c, rows, base):
    row = lax.broadcasted_iota(jnp.int32, (rows, B), 0) + base < r
    col = lax.broadcasted_iota(jnp.int32, (rows, B), 1) < c
    return row, col


def gather(v, part, s, r, c, pup):
    halves = []
    for k1 in range(2):
        a = k1 * H
        row, col = masks(r, c, H, a)
        top = jnp.where(col, v[part, a:a + H, B:T], v[part, a:a + H, 0:B])
        bot = jnp.where(col, v[part, B + a:B + a + H, B:T], v[part, B + a:B + a + H, 0:B])
        halves.append(jnp.where(row, bot, top) * pup[s, a:a + H, :])
    return halves


def forward(v, s, r, c, pup, tab):
    re, im = gather(v, 0, s, r, c, pup), gather(v, 1, s, r, c, pup)
    rows = []
    for p in range(2):
        if p == 0:
            a = jnp.concatenate([re[0] + re[1], im[0] + im[1]], axis=0)
        else:
            a = jnp.concatenate([re[0] - re[1], im[0] - im[1]], axis=0)
        rows.append(left(tab, p, a))
    out = []
    for q in range(2):
        b = []
        for p in range(2):
            y = rows[p]
            z = y[:, :H] + y[:, H:] if q == 0 else y[:, :H] - y[:, H:]
            b.append(jnp.concatenate([z[:H], z[H:]], axis=1))
        out.append(right(tab, 2 + q, jnp.concatenate(b, axis=0)))
    return out


def backward(f, s, w, tab):
    g = []
    for q in range(2):
        wq = 2.0 * w[:, q * H:(q + 1) * H]
        g.append(right(tab, q, f[s, q] * jnp.concatenate([wq, wq], axis=1)))
    a, b = g[0] + g[1], g[0] - g[1]
    re = jnp.concatenate([a[:, :H], b[:, :H]], axis=1)
    im = jnp.concatenate([a[:, H:], b[:, H:]], axis=1)
    y = []
    for p in range(2):
        y.append(left(tab, 2 + p, jnp.concatenate([re[p * H:(p + 1) * H], im[p * H:(p + 1) * H]], axis=0)))
    plus, minus = y[0] + y[1], y[0] - y[1]
    return (plus[:H], minus[:H]), (plus[H:], minus[H:])


def deposit(out, s, r, c, pup, parts):
    for k1 in range(2):
        a = k1 * H
        row, col = masks(r, c, H, a)
        pu = pup[s, a:a + H, :]
        for part in range(2):
            x = parts[part][k1] * pu
            up, down = jnp.where(row, 0.0, x), jnp.where(row, x, 0.0)
            out[part, a:a + H, 0:B] += jnp.where(col, 0.0, up)
            out[part, a:a + H, B:T] += jnp.where(col, up, 0.0)
            out[part, B + a:B + a + H, 0:B] += jnp.where(col, 0.0, down)
            out[part, B + a:B + a + H, B:T] += jnp.where(col, down, 0.0)


def pack_edges(v, edge):
    for part in range(2):
        edge[part:part + 1, :] = v[part, 0:1, :]
        edge[2 + part:3 + part, :] = v[part, T - 1:T, :]
        edge[4 + part:5 + part, :] = jnp.transpose(v[part, :, 0:H])[0:1, :]
        edge[6 + part:7 + part, :] = jnp.transpose(v[part, :, T - H:T])[H - 1:H, :]


def laplace_to(out, get, halo, scale):
    cols = jnp.transpose(halo[...])
    row = lax.broadcasted_iota(jnp.int32, (T, T), 0)
    col = lax.broadcasted_iota(jnp.int32, (T, T), 1)
    for part in range(2):
        x = get(part)
        up = jnp.where(row == 0, halo[part:part + 1, :], pltpu.roll(x, 1, axis=0))
        down = jnp.where(row == T - 1, halo[2 + part:3 + part, :], pltpu.roll(x, T - 1, axis=0))
        lt = jnp.where(col == 0, cols[:, 4 + part:5 + part], pltpu.roll(x, 1, axis=1))
        rt = jnp.where(col == T - 1, cols[:, 6 + part:7 + part], pltpu.roll(x, T - 1, axis=1))
        out[part] = scale * (4.0 * x - ((up + down) + (lt + rt)))


def fwd0_kernel(rc, v, mask, tab, f, img, pup, edge):
    base = mask[...].astype(F32)
    pack_edges(v, edge)

    def body(s, _):
        r, c = rc[s, 0], rc[s, 1]
        rolled = pltpu.roll(pltpu.roll(base, jnp.bitwise_and(r, B - 1), axis=0), jnp.bitwise_and(c, B - 1), axis=1)
        pup[s] = rolled * rc[s, 2].astype(F32)
        z = forward(v, s, r, c, pup, tab)
        for q in range(2):
            f[s, q] = z[q]
            img[s, :, q * H:(q + 1) * H] = z[q][:, :H] * z[q][:, :H] + z[q][:, H:] * z[q][:, H:]
        return 0

    lax.fori_loop(0, S, body, 0)


def fwd_kernel(rc, v, f, pup, tab, img, edge):
    pack_edges(v, edge)

    def body(s, _):
        z = forward(v, s, rc[s, 0], rc[s, 1], pup, tab)
        for q in range(2):
            fq = f[s, q]
            img[s, :, q * H:(q + 1) * H] = 2.0 * (fq[:, :H] * z[q][:, :H] + fq[:, H:] * z[q][:, H:])
        return 0

    lax.fori_loop(0, S, body, 0)


def spread_sum(x):
    return jnp.sum(x.reshape(-1, 8, H), axis=0)


def total(a, b):
    acc = jnp.zeros((8, H), F32)
    for part in range(2):
        for i in range(0, T, 64):
            acc = acc + jnp.sum((a(part, i) * b(part, i)).reshape(8, 8, T), axis=0).reshape(8, 4, H).sum(axis=1)
    return jnp.sum(acc, axis=0, keepdims=True)


def rows_of(ref):
    return lambda part, i: ref[part, i:i + 64, :]


def adj0_kernel(rc, v, f, w, pup, tab, halo, q0):
    laplace_to(q0, lambda part: v[part], halo, -REG)

    def body(s, _):
        parts = backward(f, s, -w[s], tab)
        deposit(q0, s, rc[s, 0], rc[s, 1], pup, parts)
        return 0

    lax.fori_loop(0, S, body, 0)


def adj1_kernel(rc, v, f, w, pup, tab, halo, q1, dots):
    laplace_to(q1, lambda part: v[part], halo, REG)

    def body(s, _):
        deposit(q1, s, rc[s, 0], rc[s, 1], pup, backward(f, s, w[s], tab))
        return 0

    lax.fori_loop(0, S, body, 0)
    dots[...] = jnp.zeros((8, H), F32)
    a, b = rows_of(v), rows_of(q1)
    dots[0:1, :] = total(a, a)
    dots[1:2, :] = total(a, b)
    dots[2:3, :] = total(b, b)


def scalars(red):
    lane = jnp.sum(red[...], axis=1, keepdims=True)
    res, hah, aa = lane[0:1], lane[1:2], lane[2:3]
    alpha = res / hah
    beta = (res - 2.0 * alpha * hah + alpha * alpha * aa) / res
    return alpha, beta


def adj2_kernel(rc, red, q0, q1, f, w, pup, tab, halo0, halo1, a2, h2, dots, halo):
    alpha, beta = scalars(red)
    one = 1.0 + beta
    halo[...] = one * halo0[...] - alpha * halo1[...]
    for part in range(2):
        h2[part] = one * q0[part] - alpha * q1[part]
    laplace_to(a2, lambda part: h2[part], halo, REG)

    def body(s, _):
        deposit(a2, s, rc[s, 0], rc[s, 1], pup, backward(f, s, w[s], tab))
        return 0

    lax.fori_loop(0, S, body, 0)
    dots[...] = jnp.zeros((8, H), F32)

    def res(part, i):
        return q0[part, i:i + 64, :] - alpha * q1[part, i:i + 64, :]

    dots[0:1, :] = total(res, res)
    dots[1:2, :] = total(rows_of(h2), rows_of(a2))


def finish_kernel(red, red2, q0, q1, h2, a2, step, resid):
    alpha, _ = scalars(red)
    lane = jnp.sum(red2[...], axis=1, keepdims=True)
    alpha2 = lane[0:1] / lane[1:2]
    for part in range(2):
        step[part] = alpha * q0[part] + alpha2 * h2[part]
        resid[part] = q0[part] - alpha * q1[part] - alpha2 * a2[part]


def here():
    tx = lax.axis_index("tx")
    return tx // 4, tx % 4


def exchange_kernel(phase, slot, cap, img, edge, *rest):
    if phase == 0:
        meas, wret_o, halo_o = rest[:3]
        rest = rest[3:]
    elif phase == 1:
        wret_o, halo_o, keep = rest[:3]
        rest = rest[3:]
    else:
        red, kept, wret_o, halo_o = rest[:4]
        rest = rest[4:]
    (r1, p2, r2, wl, sb, wret, halo, sem1s, sem1r, sem2s, sem2r, sem3s, sem3r, sem4s, sem4r, hs, hr) = rest
    z, y = here()
    ty = lax.axis_index("ty")
    tx = lax.axis_index("tx")
    zd = [z if d == 0 else lax.rem(z + d, 4) for d in range(4)]
    yd = [y if d == 0 else lax.rem(y + d, 4) for d in range(4)]
    tile = [[zd[d] * 4 + y for d in range(4)], [z * 4 + yd[d] for d in range(4)]]
    across = [zd, yd]
    along = [yd, zd]
    atile = [tile[1], tile[0]]

    def tile_dev(index):
        return {"tx": index}

    edge_dev = [
        {"ty": lax.rem(ty + 7, 8)}, {"ty": lax.rem(ty + 1, 8)},
        {"tx": lax.rem(tx + 15, 16)}, {"tx": lax.rem(tx + 1, 16)},
    ]
    bar = pltpu.get_barrier_semaphore()
    for half in range(2):
        for d in range(1, 4):
            pl.semaphore_signal(bar, inc=1, device_id=tile_dev(tile[half][d]), device_id_type=MESH)
    for dev in edge_dev:
        pl.semaphore_signal(bar, inc=1, device_id=dev, device_id_type=MESH)
    pl.semaphore_wait(bar, 10)

    ecopy = []
    for i, (src, dst, dev) in enumerate([(0, 2, 0), (2, 0, 1), (4, 6, 2), (6, 4, 3)]):
        ecopy.append(pltpu.make_async_remote_copy(
            src_ref=edge.at[i], dst_ref=halo.at[dst // 2],
            send_sem=hs.at[i], recv_sem=hr.at[dst // 2], device_id=edge_dev[dev], device_id_type=MESH))
    for c in ecopy:
        c.start()

    def al(x, k):
        return pl.multiple_of(x * k, 8)

    count = S + 1 if phase == 0 else S

    def copy1(half, d, s, src):
        return pltpu.make_async_remote_copy(
            src_ref=src, dst_ref=r1.at[half, 4 - d, s], send_sem=sem1s.at[half, d, s],
            recv_sem=sem1r.at[half, 4 - d, s], device_id=tile_dev(tile[half][d]), device_id_type=MESH)

    def source(half, d, s):
        rows = pl.ds(half * H + al(across[half][d], 32), 32)
        return meas.at[rows, :] if s is None else img.at[s, rows, :]

    def send1(s, _):
        for d in (2, 1, 3):
            for half in range(2):
                copy1(half, d, s, source(half, d, s)).start()
        for half in range(2):
            rows = pl.ds(half * H + al(across[half][0], 32), 32)
            r1[half, 0, s] = img[s, rows, :]
        return 0

    lax.fori_loop(0, S, send1, 0)
    if phase == 0:
        for d in (2, 1, 3):
            for half in range(2):
                copy1(half, d, S, source(half, d, None)).start()
        for half in range(2):
            r1[half, 0, S] = meas[pl.ds(half * H + al(across[half][0], 32), 32), :]
    for half in range(2):
        for d in range(4):
            r1[half, d, S + 1] = jnp.zeros((32, B), F32)

    def wait1(s, _):
        for half in range(2):
            for d in range(1, 4):
                copy1(half, d, s, img.at[0, 0:32, :]).wait()
        return 0

    lax.fori_loop(0, count, wait1, 0)

    def partial(c, _):
        for half in range(2):
            acc = r1[half, 0, slot[tile[half][0], c]]
            for d in range(1, 4):
                acc = acc + r1[half, d, slot[tile[half][d], c]]
            p2[half, c] = acc
        return 0

    lax.fori_loop(0, N, partial, 0)
    if phase == 0:
        for half in range(2):
            for d in range(4):
                p2[half, tile[half][d]] -= r1[half, d, S]

    def copy2(half, d):
        return pltpu.make_async_remote_copy(
            src_ref=p2.at[half, :, pl.ds(al(along[half][d], 8), 8), :], dst_ref=r2.at[half, 4 - d],
            send_sem=sem2s.at[half, d], recv_sem=sem2r.at[half, 4 - d],
            device_id=tile_dev(atile[half][d]), device_id_type=MESH)

    for d in (2, 1, 3):
        for half in range(2):
            copy2(half, d).start()
    for d in (2, 1, 3):
        for half in range(2):
            copy2(half, d).wait()
    for half in range(2):
        mine = pl.ds(al(along[half][0], 8), 8)
        w = p2[half, :, mine, :] + r2[half, 1] + (r2[half, 2] + r2[half, 3])
        if phase == 1:
            keep[half] = w
        if phase == 2:
            alpha, beta = scalars(red)
            w = (1.0 + beta)[0, 0] * kept[half] - alpha[0, 0] * w
        wl[half, :, mine, :] = w

    def copy3(half, d):
        mine = pl.ds(al(along[half][0], 8), 8)
        return pltpu.make_async_remote_copy(
            src_ref=wl.at[half, :, mine, :], dst_ref=wl.at[half, :, mine, :],
            send_sem=sem3s.at[half, d], recv_sem=sem3r.at[half, 4 - d],
            device_id=tile_dev(atile[half][d]), device_id_type=MESH)

    for d in (2, 1, 3):
        for half in range(2):
            copy3(half, d).start()
    for d in (2, 1, 3):
        for half in range(2):
            c = copy3(half, d)
            c.wait_send()
            from_rows = pl.ds(al(along[half][4 - d], 8), 8)
            pltpu.make_async_remote_copy(
                src_ref=wl.at[half, :, from_rows, :], dst_ref=wl.at[half, :, from_rows, :],
                send_sem=sem3s.at[half, d], recv_sem=sem3r.at[half, 4 - d],
                device_id=tile_dev(atile[half][d]), device_id_type=MESH).wait_recv()

    def copy4(half, d, s, owner):
        rows = pl.ds(half * H + al(across[half][owner], 32), 32)
        return pltpu.make_async_remote_copy(
            src_ref=sb.at[half, d, s], dst_ref=wret.at[s, rows, :], send_sem=sem4s.at[half, d, s],
            recv_sem=sem4r.at[half, 4 - d, s], device_id=tile_dev(tile[half][d]), device_id_type=MESH)

    def send4(s, _):
        for d in (2, 1, 3):
            for half in range(2):
                sb[half, d, s] = wl[half, cap[tile[half][d], s]]
                copy4(half, d, s, 0).start()
        for half in range(2):
            rows = pl.ds(half * H + al(across[half][0], 32), 32)
            wret[s, rows, :] = wl[half, cap[tile[half][0], s]]
        return 0

    lax.fori_loop(0, S, send4, 0)

    def wait4(s, _):
        for half in range(2):
            for d in range(1, 4):
                copy4(half, d, s, 0).wait_send()
                copy4(half, d, s, 4 - d).wait_recv()
        return 0

    lax.fori_loop(0, S, wait4, 0)
    for c in ecopy:
        c.wait()

    def out(s, _):
        wret_o[s] = wret[s]
        return 0

    lax.fori_loop(0, S, out, 0)
    for i, edge_on in enumerate((ty > 0, ty < 7, tx > 0, tx < 15)):
        halo_o[i] = jnp.where(edge_on, halo[i], 0.0)


def reduce_kernel(x, out, rx, ry, mid, ss, rs, ss2, rs2):
    ty, tx = lax.axis_index("ty"), lax.axis_index("tx")
    bar = pltpu.get_barrier_semaphore()
    for d in range(1, 16):
        pl.semaphore_signal(bar, inc=1, device_id={"tx": lax.rem(tx + d, 16)}, device_id_type=MESH)
    for d in range(1, 8):
        pl.semaphore_signal(bar, inc=1, device_id={"ty": lax.rem(ty + d, 8)}, device_id_type=MESH)
    pl.semaphore_wait(bar, 22)
    copies = [pltpu.make_async_remote_copy(
        src_ref=x, dst_ref=rx.at[d], send_sem=ss.at[d], recv_sem=rs.at[d],
        device_id={"tx": lax.rem(tx + d, 16)}, device_id_type=MESH) for d in range(1, 16)]
    for c in copies:
        c.start()
    for c in copies:
        c.wait()
    acc = x[...]
    for d in range(1, 16):
        acc = acc + rx[d]
    mid[...] = acc
    copies = [pltpu.make_async_remote_copy(
        src_ref=mid, dst_ref=ry.at[d], send_sem=ss2.at[d], recv_sem=rs2.at[d],
        device_id={"ty": lax.rem(ty + d, 8)}, device_id_type=MESH) for d in range(1, 8)]
    for c in copies:
        c.start()
    for c in copies:
        c.wait()
    acc = mid[...]
    for d in range(1, 8):
        acc = acc + ry[d]
    out[...] = acc


def sds(*shape):
    return jax.ShapeDtypeStruct(shape, F32)


def call(kernel, ins, outs, scratch=(), cid=None, name=None):
    params = dict(vmem_limit_bytes=62 << 20)
    if cid is not None:
        params.update(collective_id=cid, has_side_effects=True)
    specs = [SM if x.dtype == jnp.int32 and x.shape != (B, B) else VM for x in ins]
    return pl.pallas_call(
        kernel, out_shape=outs, in_specs=specs, out_specs=[VM] * len(outs), scratch_shapes=list(scratch),
        compiler_params=pltpu.CompilerParams(**params), name=name)(*ins)


def exchange(phase, ins, outs):
    dma = pltpu.SemaphoreType.DMA
    scratch = [
        pltpu.VMEM((2, 4, S + 2, 32, B), F32), pltpu.VMEM((2, N, 32, B), F32), pltpu.VMEM((2, 4, N, 8, B), F32),
        pltpu.VMEM((2, N, 32, B), F32), pltpu.VMEM((2, 4, S, 32, B), F32), pltpu.VMEM((S, B, B), F32),
        pltpu.VMEM((4, 2, T), F32),
        dma((2, 4, S + 1)), dma((2, 4, S + 1)), dma((2, 4)), dma((2, 4)), dma((2, 4)), dma((2, 4)),
        dma((2, 4, S)), dma((2, 4, S)), dma((4,)), dma((4,)),
    ]
    return call(lambda *refs: exchange_kernel(phase, *refs), ins, outs, scratch, cid=phase, name="exchange%d" % phase)


def all_sum(x, cid):
    dma = pltpu.SemaphoreType.DMA
    scratch = [pltpu.VMEM((16, 8, H), F32), pltpu.VMEM((8, 8, H), F32), pltpu.VMEM((8, H), F32),
               dma((16,)), dma((16,)), dma((8,)), dma((8,))]
    return call(reduce_kernel, [x], [sds(8, H)], scratch, cid=cid, name="allsum%d" % cid)[0]


def routes(led_count, led_owner, led_offset):
    row = lax.axis_index("ty") * N
    column = lax.axis_index("tx")
    owner = lax.dynamic_slice_in_dim(led_owner, row, N, 0)
    count = lax.dynamic_slice_in_dim(led_count, row, N, 0)
    offset = lax.dynamic_slice_in_dim(led_offset, row, N, 0)
    slots = jnp.arange(S, dtype=jnp.int32)
    ids = jnp.arange(N, dtype=jnp.int32)
    live = slots[None, :] < count[:, None]
    hit = (owner[:, :, None] == ids[None, None, :]) & live[:, :, None]
    served = jnp.sum(hit.astype(jnp.int32), axis=1)
    rank = jnp.sum(served[None, :, :] * (ids[None, :, None] < ids[:, None, None]).astype(jnp.int32), axis=1)
    slot = jnp.where(served > 0, rank, S + 1).T
    chosen = (served[:, :, None] > 0) & (rank[:, :, None] == slots[None, None, :])
    cap = jnp.sum(jnp.where(chosen, ids[:, None, None], 0), axis=0)
    mine = lax.dynamic_slice_in_dim(chosen.astype(jnp.int32), column, 1, 1)[:, 0]
    own = lax.dynamic_slice_in_dim(hit.astype(jnp.int32), column, 1, 2)
    corner = jnp.sum(own * offset, axis=1)
    rc = jnp.sum(mine[:, :, None] * corner[:, None, :], axis=0)
    rc = jnp.concatenate([rc, jnp.sum(mine, axis=0)[:, None]], axis=1)
    return slot, cap, rc


def on_device(spectrum, measured, pupil_mask, led_count, led_owner, led_offset):
    highest = lax.Precision.HIGHEST
    slot, cap, rc = routes(led_count, led_owner, led_offset)
    tab = tables()
    pick = np.zeros((B, B), np.float32)
    for p in range(2):
        pick[p * H + np.arange(H), 2 * np.arange(H) + p] = 1.0
    pick = jnp.asarray(pick)
    meas = jnp.dot(jnp.dot(pick, measured[0], precision=highest), pick.T, precision=highest)

    f, img, pup, edge = call(fwd0_kernel, [rc, spectrum, pupil_mask, tab],
                             [sds(S, 2, B, B), sds(S, B, B), sds(S, B, B), sds(8, T)], name="fwd0")
    w, halo = exchange(0, [slot, cap, img, edge.reshape(4, 2, T), meas], [sds(S, B, B), sds(4, 2, T)])
    q0, = call(adj0_kernel, [rc, spectrum, f, w, pup, tab, halo.reshape(8, T)], [sds(2, T, T)], name="adj0")
    img, edge = call(fwd_kernel, [rc, q0, f, pup, tab], [sds(S, B, B), sds(8, T)], name="fwd1")
    w, halo0, keep = exchange(1, [slot, cap, img, edge.reshape(4, 2, T)],
                              [sds(S, B, B), sds(4, 2, T), sds(2, N, 8, B)])
    halo0 = halo0.reshape(8, T)
    q1, dots = call(adj1_kernel, [rc, q0, f, w, pup, tab, halo0], [sds(2, T, T), sds(8, H)], name="adj1")
    red = all_sum(dots, 3)
    img, edge = call(fwd_kernel, [rc, q1, f, pup, tab], [sds(S, B, B), sds(8, T)], name="fwd2")
    w, halo1 = exchange(2, [slot, cap, img, edge.reshape(4, 2, T), red, keep], [sds(S, B, B), sds(4, 2, T)])
    a2, h2, dots = call(adj2_kernel, [rc, red, q0, q1, f, w, pup, tab, halo0, halo1.reshape(8, T)],
                        [sds(2, T, T), sds(2, T, T), sds(8, H)], [pltpu.VMEM((8, T), F32)], name="adj2")
    red2 = all_sum(dots, 4)
    step, resid = call(finish_kernel, [red, red2, q0, q1, h2, a2], [sds(2, T, T), sds(2, T, T)], name="finish")
    return step, resid


def solution(mesh):
    placed = (P(None, "ty", "tx"), P(("ty", "tx"), None, None), P(), P(), P(), P())
    return jax.shard_map(
        on_device, mesh=mesh, in_specs=placed,
        out_specs=(P(None, "ty", "tx"), P(None, "ty", "tx")), check_vma=False)
```

time: 1160 us -> 292 us (0.25)
  blocking collectives: 308 us -> 0 us
  Pallas kernels: 0 us -> 273 us
  matrix products: 263 us -> 3.38 us
  waiting for transfers between devices: 187 us -> 0 us
  local copies, waits for them, and re-layouts: 180 us -> 9.84 us
  other arithmetic: 112 us -> 3.49 us
  starting transfers between devices: 60.8 us -> 0 us
  between operations: 35.9 us -> 0.74 us
    pallas_call x0 -> x12, Pallas kernels: none -> 273 us  [call(): pl.pallas_call(kernel, out_shape=outs, in_specs=specs, out_specs=[VM] * l...]
    dot_general x54 -> x2, matrix products: 263 us -> 3.38 us  [the longest x1 2.05 us: on_device(): jnp.dot(jnp.dot(pick, measured[0], precision=highest), pick.T, precision=...]
    psum x3 -> x0, blocking collectives: 201 us -> none  [the longest x2 136 us: squared(): return lax.psum(jnp.sum(values * values), ('ty', 'tx'))]
    dynamic_update_slice x24 -> x0, local copies, waits for them, and re-layouts: 150 us -> none  [adjoint(): lax.dynamic_update_slice(deposit, window + contrib[slot_no], corner)]
    ppermute x12 -> x0, waiting for transfers between devices: 118 us -> none  [the longest x6 115 us: extended(): after = lax.ppermute(initial, axis, down)]
    all_to_all x2 -> x0, blocking collectives: 107 us -> none  [to_capture(): lax.all_to_all(dest_term, 'tx', split_axis=0, concat_axis=0, tiled=True)]
    all_to_all x4 -> x0, waiting for transfers between devices: 69.8 us -> none  [the longest x1 62 us: to_capture(): lax.all_to_all(dest_term, 'tx', split_axis=0, concat_axis=0, tiled=True)]
    add x22 -> x0, other arithmetic: 50.9 us -> none  [the longest x21 48.2 us: adjoint(): window + contrib[slot_no]]
  transfers between devices with their start and end apart: 16 -> 0, of which waited for: 10 -> 0; matrix products, arithmetic and copies ran while one was open for 1% -> 0% of each run, Pallas kernels for 0% -> 0%
where the time goes in v1:
time: 292 us; the launch traced here: 291 us
  Pallas kernels  273 us (93%)
  local copies, waits for them, and re-layouts  9.84 us (3%)
  other arithmetic  3.49 us (1%)
  matrix products  3.38 us (1%)
    pallas_call x12, Pallas kernels, call(): pl.pallas_call(kernel, out_shape=outs, in_specs=specs, out_specs=[VM] * l...  273 us

profile of v1, /device:TPU:1, one launch (start us, length us, event | category | flops | bytes accessed | tf_op | source)
XLA Modules:
  0.0 290.7 jit_solution(10753304601943254697)
XLA Ops:
  0.7 0.8 dynamic_slice.16
  1.4 0.8 constant_dynamic-slice_fusion
  3.1 0.9 select_reduce_fusion.refs_1_
  4.3 0.8 multiply_reduce_fusion.2
  6.0 1.3 fusion
  7.4 2.1 fusion.7.refs_4_
  9.4 13.0 %fwd0.1 = (f32[8,2,256,256]{3,2,1,0:T(8,128)}, f32[8,256,256]{2,1,0:T(8,128)}, f32[8,256,256]{2,1,0:T(8,128)}, f32[8,512]{1,0:T(8,128)}) custom-call(s32[8,3]{1,0:T(8,128)} %pad_add_fusion.rc, f32[2,512,512]{2,1,0:T(8,128)} %v.3, s32[256,256]{1,0:T(8,128)} %mask.1, bf16[2,4,256,256]{3,2,1,0:T(8,128)(2,1)} %constant.23.clone.tab), custom_call_target="tpu_custom_call" | custom-call | tf_op jit(solution)/shard_map/fwd0/pallas_call | solution.py:478
  22.4 1.3 reshape.69.refs_3_
  23.8 55.3 %exchange0.1 = (f32[8,256,256]{2,1,0:T(8,128)}, f32[4,2,512]{2,1,0:T(2,128)}) custom-call(s32[16,16]{1,0:T(8,128)} %get-tuple-element.42.refs_0_, s32[16,8]{1,0:T(8,128)} %select_reduce_fusion.refs_1_, f32[8,256,256]{2,1,0:T(8,128)} %get-tuple-element.23.refs_2_, f32[4,2,512]{2,1,0:T(2,128)} %reshape.69.refs_3_, f32[256,256]{1,0:T(8,128)} %fusion.7.refs_4_), custom_call_target="tpu_custom_call" | custom-call | tf_op jit(solution)/shard_map/exchange0/pallas_call | solution.py:478
  79.0 1.3 reshape.70.halo
  80.4 14.7 %adj0.1.v.q0 = f32[2,512,512]{2,1,0:T(8,128)} custom-call(s32[8,3]{1,0:T(8,128)} %pad_add_fusion.rc, f32[2,512,512]{2,1,0:T(8,128)} %v.3, f32[8,2,256,256]{3,2,1,0:T(8,128)} %get-tuple-element.22.f, f32[8,256,256]{2,1,0:T(8,128)} %get-tuple-element.25.w, f32[8,256,256]{2,1,0:T(8,128)} %get-tuple-element.26.pup, bf16[2,4,256,256]{3,2,1,0:T(8,128)(2,1)} %constant.23.clone.tab, ...), custom_call_target="tpu_custom_call" | custom-call | tf_op jit(solution)/shard_map/adj0/pallas_call | solution.py:478
  95.0 11.7 %fwd1.1 = (f32[8,256,256]{2,1,0:T(8,128)}, f32[8,512]{1,0:T(8,128)}) custom-call(s32[8,3]{1,0:T(8,128)} %pad_add_fusion.rc, f32[2,512,512]{2,1,0:T(8,128)} %adj0.1.v.q0, f32[8,2,256,256]{3,2,1,0:T(8,128)} %get-tuple-element.22.f, f32[8,256,256]{2,1,0:T(8,128)} %get-tuple-element.26.pup, bf16[2,4,256,256]{3,2,1,0:T(8,128)(2,1)} %constant.23.clone.tab), custom_call_target="tpu_custom_call" | custom-call | tf_op jit(solution)/shard_map/fwd1/pallas_call | solution.py:478
  106.7 1.3 reshape.71.refs_3_
  108.0 51.6 %exchange1.1 = (f32[8,256,256]{2,1,0:T(8,128)}, f32[4,2,512]{2,1,0:T(2,128)}, f32[2,16,8,256]{3,2,1,0:T(8,128)}) custom-call(s32[16,16]{1,0:T(8,128)} %get-tuple-element.42.refs_0_, s32[16,8]{1,0:T(8,128)} %select_reduce_fusion.refs_1_, f32[8,256,256]{2,1,0:T(8,128)} %get-tuple-element.28.refs_2_, f32[4,2,512]{2,1,0:T(2,128)} %reshape.71.refs_3_), custom_call_target="tpu_custom_call" | custom-call | tf_op jit(solution)/shard_map/exchange1/pallas_call | solution.py:478
  159.7 1.3 reshape.72.halo.halo0
  161.0 14.9 %adj1.1 = (f32[2,512,512]{2,1,0:T(8,128)}, f32[8,128]{1,0:T(8,128)}) custom-call(s32[8,3]{1,0:T(8,128)} %pad_add_fusion.rc, f32[2,512,512]{2,1,0:T(8,128)} %adj0.1.v.q0, f32[8,2,256,256]{3,2,1,0:T(8,128)} %get-tuple-element.22.f, f32[8,256,256]{2,1,0:T(8,128)} %get-tuple-element.30.w, f32[8,256,256]{2,1,0:T(8,128)} %get-tuple-element.26.pup, ...), custom_call_target="tpu_custom_call" | custom-call | tf_op jit(solution)/shard_map/adj1/pallas_call | solution.py:478
  175.9 13.8 %allsum3.1.refs_4_.red = f32[8,128]{1,0:T(8,128)} custom-call(f32[8,128]{1,0:T(8,128)} %get-tuple-element.32.x), custom_call_target="tpu_custom_call" | custom-call | tf_op jit(solution)/shard_map/allsum3/pallas_call | solution.py:478
  189.7 11.7 %fwd2.1 = (f32[8,256,256]{2,1,0:T(8,128)}, f32[8,512]{1,0:T(8,128)}) custom-call(s32[8,3]{1,0:T(8,128)} %pad_add_fusion.rc, f32[2,512,512]{2,1,0:T(8,128)} %get-tuple-element.33.v.q1, f32[8,2,256,256]{3,2,1,0:T(8,128)} %get-tuple-element.22.f, f32[8,256,256]{2,1,0:T(8,128)} %get-tuple-element.26.pup, bf16[2,4,256,256]{3,2,1,0:T(8,128)(2,1)} %constant.23.clone.tab), custom_call_target="tpu_custom_call" | custom-call | tf_op jit(solution)/shard_map/fwd2/pallas_call | solution.py:478
  201.4 1.3 reshape.73.refs_3_
  202.8 50.8 %exchange2.1 = (f32[8,256,256]{2,1,0:T(8,128)}, f32[4,2,512]{2,1,0:T(2,128)}) custom-call(s32[16,16]{1,0:T(8,128)} %get-tuple-element.42.refs_0_, s32[16,8]{1,0:T(8,128)} %select_reduce_fusion.refs_1_, f32[8,256,256]{2,1,0:T(8,128)} %get-tuple-element.34.refs_2_, f32[4,2,512]{2,1,0:T(2,128)} %reshape.73.refs_3_, f32[8,128]{1,0:T(8,128)} %allsum3.1.refs_4_.red, ...), custom_call_target="tpu_custom_call" | custom-call | tf_op jit(solution)/shard_map/exchange2/pallas_call | solution.py:478
  253.6 1.3 reshape.74.halo1
  254.9 15.7 %adj2.1 = (f32[2,512,512]{2,1,0:T(8,128)}, f32[2,512,512]{2,1,0:T(8,128)}, f32[8,128]{1,0:T(8,128)}) custom-call(s32[8,3]{1,0:T(8,128)} %pad_add_fusion.rc, f32[8,128]{1,0:T(8,128)} %allsum3.1.refs_4_.red, f32[2,512,512]{2,1,0:T(8,128)} %adj0.1.v.q0, f32[2,512,512]{2,1,0:T(8,128)} %get-tuple-element.33.v.q1, f32[8,2,256,256]{3,2,1,0:T(8,128)} %get-tuple-element.22.f, ...), custom_call_target="tpu_custom_call" | custom-call | tf_op jit(solution)/shard_map/adj2/pallas_call | solution.py:478
  270.6 13.7 %allsum4.1.red2 = f32[8,128]{1,0:T(8,128)} custom-call(f32[8,128]{1,0:T(8,128)} %get-tuple-element.39.x), custom_call_target="tpu_custom_call" | custom-call | tf_op jit(solution)/shard_map/allsum4/pallas_call | solution.py:478
  284.3 6.4 %finish.1 = (f32[2,512,512]{2,1,0:T(8,128)}, f32[2,512,512]{2,1,0:T(8,128)}) custom-call(f32[8,128]{1,0:T(8,128)} %allsum3.1.refs_4_.red, f32[8,128]{1,0:T(8,128)} %allsum4.1.red2, f32[2,512,512]{2,1,0:T(8,128)} %adj0.1.v.q0, f32[2,512,512]{2,1,0:T(8,128)} %get-tuple-element.33.v.q1, f32[2,512,512]{2,1,0:T(8,128)} %get-tuple-element.40.h2, ...), custom_call_target="tpu_custom_call" | custom-call | tf_op jit(solution)/shard_map/finish/pallas_call | solution.py:478
  (18 shorter events, 2.1 us)
Async XLA Ops:
  0.6 5.4 %copy-start = (f32[1,256,256]{2,1,0:T(8,128)S(1)}, f32[1,256,256]{2,1,0:T(8,128)}, u32[]{:S(2)}) copy-start(f32[1,256,256]{2,1,0:T(8,128)} %param.9) | copy-start | bytes 786436

commit v2 on v0

v2 whole, which is shorter than its diff:
```python
import jax
import jax.numpy as jnp
import numpy as np
from jax import lax
from jax.experimental import pallas as pl
from jax.experimental.pallas import tpu as pltpu
from jax.sharding import PartitionSpec as P

B = 256
H = 128
T = 512
S = 8
N = 16
REG = 0.5
F32 = jnp.float32
BF = jnp.bfloat16
MESH = pl.DeviceIdType.MESH
VM = pl.BlockSpec(memory_space=pltpu.VMEM)
SM = pl.BlockSpec(memory_space=pltpu.SMEM)


def tables():
    m = np.arange(H)
    out = []
    for p in range(2):
        ang = ((2 * m[:, None] + p) * m[None, :] % B) * (2.0 * np.pi / B)
        re, im = np.cos(ang) / 16.0, np.sin(ang) / 16.0
        out.append(np.block([[re, -im], [im, re]]))
    full = np.stack([out[0], out[1], out[0].T, out[1].T])
    hi = full.astype(np.float32).astype(jnp.bfloat16)
    lo = (full - hi.astype(np.float64)).astype(np.float32).astype(jnp.bfloat16)
    return jnp.asarray(np.stack([hi, lo]))


def split(x):
    hi = x.astype(BF)
    return hi, (x - hi.astype(F32)).astype(BF)


def mm(a, b):
    return jnp.dot(a, b, preferred_element_type=F32)


def left(tab, k, x):
    hi, lo = split(x)
    return mm(tab[0, k], hi) + (mm(tab[0, k], lo) + mm(tab[1, k], hi))


def right(tab, k, x):
    hi, lo = split(x)
    return mm(hi, tab[0, k]) + (mm(lo, tab[0, k]) + mm(hi, tab[1, k]))


def masks(r, c, rows, base):
    row = lax.broadcasted_iota(jnp.int32, (rows, B), 0) + base < r
    col = lax.broadcasted_iota(jnp.int32, (rows, B), 1) < c
    return row, col


def gather(v, part, s, r, c, pup):
    halves = []
    for k1 in range(2):
        a = k1 * H
        row, col = masks(r, c, H, a)
        top = jnp.where(col, v[part, a:a + H, B:T], v[part, a:a + H, 0:B])
        bot = jnp.where(col, v[part, B + a:B + a + H, B:T], v[part, B + a:B + a + H, 0:B])
        halves.append(jnp.where(row, bot, top) * pup[s, a:a + H, :])
    return halves


def forward(v, s, r, c, pup, tab):
    re, im = gather(v, 0, s, r, c, pup), gather(v, 1, s, r, c, pup)
    rows = []
    for p in range(2):
        if p == 0:
            a = jnp.concatenate([re[0] + re[1], im[0] + im[1]], axis=0)
        else:
            a = jnp.concatenate([re[0] - re[1], im[0] - im[1]], axis=0)
        rows.append(left(tab, p, a))
    out = []
    for q in range(2):
        b = []
        for p in range(2):
            y = rows[p]
            z = y[:, :H] + y[:, H:] if q == 0 else y[:, :H] - y[:, H:]
            b.append(jnp.concatenate([z[:H], z[H:]], axis=1))
        out.append(right(tab, 2 + q, jnp.concatenate(b, axis=0)))
    return out


def backward(f, s, w, tab):
    g = []
    for q in range(2):
        wq = 2.0 * w[:, q * H:(q + 1) * H]
        g.append(right(tab, q, f[s, q] * jnp.concatenate([wq, wq], axis=1)))
    a, b = g[0] + g[1], g[0] - g[1]
    re = jnp.concatenate([a[:, :H], b[:, :H]], axis=1)
    im = jnp.concatenate([a[:, H:], b[:, H:]], axis=1)
    y = []
    for p in range(2):
        y.append(left(tab, 2 + p, jnp.concatenate([re[p * H:(p + 1) * H], im[p * H:(p + 1) * H]], axis=0)))
    plus, minus = y[0] + y[1], y[0] - y[1]
    return (plus[:H], minus[:H]), (plus[H:], minus[H:])


def deposit(out, s, r, c, pup, parts):
    for k1 in range(2):
        a = k1 * H
        row, col = masks(r, c, H, a)
        pu = pup[s, a:a + H, :]
        for part in range(2):
            x = parts[part][k1] * pu
            up, down = jnp.where(row, 0.0, x), jnp.where(row, x, 0.0)
            out[part, a:a + H, 0:B] += jnp.where(col, 0.0, up)
            out[part, a:a + H, B:T] += jnp.where(col, up, 0.0)
            out[part, B + a:B + a + H, 0:B] += jnp.where(col, 0.0, down)
            out[part, B + a:B + a + H, B:T] += jnp.where(col, down, 0.0)


def pack_edges(v, edge):
    for part in range(2):
        edge[0, part:part + 1, :] = v[part, 0:1, :]
        edge[1, part:part + 1, :] = v[part, T - 1:T, :]
        edge[2, part:part + 1, :] = jnp.transpose(v[part, :, 0:H])[0:1, :]
        edge[3, part:part + 1, :] = jnp.transpose(v[part, :, T - H:T])[H - 1:H, :]


def laplace_to(out, v, halo, scale):
    row = lax.broadcasted_iota(jnp.int32, (T, T), 0)
    col = lax.broadcasted_iota(jnp.int32, (T, T), 1)
    lcol, rcol = jnp.transpose(halo[2]), jnp.transpose(halo[3])
    for part in range(2):
        x = v[part]
        up = jnp.where(row == 0, halo[0, part:part + 1, :], pltpu.roll(x, 1, axis=0))
        down = jnp.where(row == T - 1, halo[1, part:part + 1, :], pltpu.roll(x, T - 1, axis=0))
        lt = jnp.where(col == 0, lcol[:, part:part + 1], pltpu.roll(x, 1, axis=1))
        rt = jnp.where(col == T - 1, rcol[:, part:part + 1], pltpu.roll(x, T - 1, axis=1))
        out[part] = scale * (4.0 * x - ((up + down) + (lt + rt)))


def lanes(x):
    one = jnp.sum(x, axis=0, keepdims=True)
    acc = one[:, 0:H]
    for i in range(H, x.shape[1], H):
        acc = acc + one[:, i:i + H]
    return acc


def dot_rows(a, b):
    acc = jnp.zeros((1, H), F32)
    for part in range(2):
        acc = acc + lanes(a(part) * b(part))
    return acc


def whole(ref):
    return lambda part: ref[part]


def kernel(slot, cap, rc, spectrum, mask, meas, tab, step, resid,
           f, pup, img, r1, p2, r2, wl, sb, wret, keep, edge, halo, q0, q1, h2, ax, arx, ary, amid,
           sem, sem4, asem):
    tx, ty = lax.axis_index("tx"), lax.axis_index("ty")
    z, y = tx // 4, tx % 4
    zd = [z] + [lax.rem(z + d, 4) for d in range(1, 4)]
    yd = [y] + [lax.rem(y + d, 4) for d in range(1, 4)]
    tile = [[zd[d] * 4 + y for d in range(4)], [z * 4 + yd[d] for d in range(4)]]
    across, along, atile = [zd, yd], [yd, zd], [tile[1], tile[0]]
    tx_dev = [{"tx": lax.rem(tx + d, 16)} for d in range(16)]
    ty_dev = [{"ty": lax.rem(ty + d, 8)} for d in range(8)]
    edge_dev = [ty_dev[7], ty_dev[1], tx_dev[15], tx_dev[1]]

    def remote(src, dst, send, recv, dev):
        return pltpu.make_async_remote_copy(
            src_ref=src, dst_ref=dst, send_sem=send, recv_sem=recv, device_id=dev, device_id_type=MESH)

    def wait_sent(ref, s):
        remote(ref, ref, s, s, tx_dev[1]).wait_send()

    def wait_got(ref, s):
        remote(ref, ref, s, s, tx_dev[1]).wait_recv()

    def al(x, k):
        return pl.multiple_of(x * k, 8)

    def line_rows(half, d):
        return pl.ds(half * H + al(across[half][d], 32), 32)

    def sum_start(k):
        for d in range(1, 16):
            remote(ax.at[k], arx.at[k, d], asem.at[k, 0], asem.at[k, 1], tx_dev[d]).start()

    def sum_turn(k):
        wait_sent(arx.at[k, 1:16], asem.at[k, 0])
        wait_got(arx.at[k, 1:16], asem.at[k, 1])
        acc = ax[k]
        for d in range(1, 16):
            acc = acc + arx[k, d]
        amid[k] = acc
        for d in range(1, 8):
            remote(amid.at[k], ary.at[k, d], asem.at[k, 2], asem.at[k, 3], ty_dev[d]).start()

    def sum_end(k):
        wait_sent(ary.at[k, 1:8], asem.at[k, 2])
        wait_got(ary.at[k, 1:8], asem.at[k, 3])
        acc = amid[k]
        for d in range(1, 8):
            acc = acc + ary[k, d]
        return jnp.sum(acc, axis=1, keepdims=True)

    def halo_start(ph, v):
        pack_edges(v, edge.at[ph])
        for i, dst in enumerate((1, 0, 3, 2)):
            remote(edge.at[ph, i], halo.at[ph, dst], sem.at[ph, 0], sem.at[ph, 1], edge_dev[i]).start()

    def halo_end(ph):
        wait_sent(edge.at[ph], sem.at[ph, 0])
        wait_got(halo.at[ph], sem.at[ph, 1])
        for i, inside in enumerate((ty > 0, ty < 7, tx > 0, tx < 15)):
            halo[ph, i] = jnp.where(inside, halo[ph, i], 0.0)

    def send1(ph, s):
        for d in (2, 1, 3):
            for half in range(2):
                remote(img.at[s, line_rows(half, d), :], r1.at[ph, half, 4 - d, s],
                       sem.at[ph, 2], sem.at[ph, 3], {"tx": tile[half][d]}).start()
        for half in range(2):
            r1[ph, half, 0, s] = img[s, line_rows(half, 0), :]

    def sums(ph):
        wait_sent(img.at[0:6], sem.at[ph, 2])
        wait_got(r1.at[ph, :, 1:4, 0:S], sem.at[ph, 3])
        if ph == 0:
            wait_sent(r1.at[ph, :, 1:4, S], sem.at[ph, 10])
            wait_got(r1.at[ph, :, 1:4, S], sem.at[ph, 11])

        def partial(c, _):
            for half in range(2):
                acc = r1[ph, half, 0, slot[tile[half][0], c]]
                for d in range(1, 4):
                    acc = acc + r1[ph, half, d, slot[tile[half][d], c]]
                p2[half, c] = acc
            return 0

        lax.fori_loop(0, N, partial, 0)
        if ph == 0:
            for half in range(2):
                for d in range(4):
                    p2[half, tile[half][d]] -= r1[ph, half, d, S]
        for d in (2, 1, 3):
            for half in range(2):
                remote(p2.at[half, :, pl.ds(al(along[half][d], 8), 8), :], r2.at[ph, half, 4 - d],
                       sem.at[ph, 4], sem.at[ph, 5], {"tx": atile[half][d]}).start()

    def mine(half):
        return pl.ds(al(along[half][0], 8), 8)

    def sums_end(ph, fix):
        wait_sent(r2.at[ph, :, 1:4], sem.at[ph, 4])
        wait_got(r2.at[ph, :, 1:4], sem.at[ph, 5])
        for half in range(2):
            w = (p2[half, :, mine(half), :] + r2[ph, half, 1]) + (r2[ph, half, 2] + r2[ph, half, 3])
            wl[ph, half, :, mine(half), :] = fix(half, w)
        for d in (2, 1, 3):
            for half in range(2):
                part = wl.at[ph, half, :, mine(half), :]
                remote(part, part, sem.at[ph, 6], sem.at[ph, 7], {"tx": atile[half][d]}).start()

    def give_back(ph):
        wait_sent(wl.at[ph, :, :, 0:24, :], sem.at[ph, 6])
        wait_got(wl.at[ph, :, :, 0:24, :], sem.at[ph, 7])

        def send4(s, _):
            for d in (2, 1, 3):
                for half in range(2):
                    sb[half, d - 1, s] = wl[ph, half, cap[tile[half][d], s]]
                    remote(sb.at[half, d - 1, s], wret.at[ph, s, line_rows(half, 0), :],
                           sem.at[ph, 8], sem4.at[ph, s], {"tx": tile[half][d]}).start()
            for half in range(2):
                wret[ph, s, line_rows(half, 0), :] = wl[ph, half, cap[tile[half][0], s]]
            return 0

        lax.fori_loop(0, S, send4, 0)

    def adjoint(ph, out, sign):
        def body(s, _):
            wait_got(wret.at[ph, s, 0:192, :], sem4.at[ph, s])
            w = wret[ph, s]
            deposit(out, s, rc[s, 0], rc[s, 1], pup, backward(f, s, -w if sign < 0 else w, tab))
            return 0

        lax.fori_loop(0, S, body, 0)
        wait_sent(sb, sem.at[ph, 8])

    bar = pltpu.get_barrier_semaphore()
    for dev in tx_dev[1:] + ty_dev[1:]:
        pl.semaphore_signal(bar, inc=1, device_id=dev, device_id_type=MESH)
    for ph in range(3):
        for half in range(2):
            for d in range(4):
                r1[ph, half, d, S + 1] = jnp.zeros((32, B), F32)
    pl.semaphore_wait(bar, 22)

    for d in (2, 1, 3):
        for half in range(2):
            remote(meas.at[line_rows(half, d), :], r1.at[0, half, 4 - d, S],
                   sem.at[0, 10], sem.at[0, 11], {"tx": tile[half][d]}).start()
    for half in range(2):
        r1[0, half, 0, S] = meas[line_rows(half, 0), :]
    halo_start(0, spectrum)

    def fields(s, _):
        r, c = rc[s, 0], rc[s, 1]
        base = mask[...].astype(F32)
        rolled = pltpu.roll(pltpu.roll(base, jnp.bitwise_and(r, B - 1), axis=0), jnp.bitwise_and(c, B - 1), axis=1)
        pup[s] = rolled * rc[s, 2].astype(F32)
        g = forward(spectrum, s, r, c, pup, tab)
        for q in range(2):
            f[s, q] = g[q]
            img[s, :, q * H:(q + 1) * H] = g[q][:, :H] * g[q][:, :H] + g[q][:, H:] * g[q][:, H:]
        send1(0, s)
        return 0

    lax.fori_loop(0, S, fields, 0)
    halo_end(0)
    laplace_to(q0, spectrum, halo.at[0], -REG)
    sums(0)
    sums_end(0, lambda half, w: w)
    give_back(0)
    adjoint(0, q0, -1)

    def images(ph, v):
        def body(s, _):
            g = forward(v, s, rc[s, 0], rc[s, 1], pup, tab)
            for q in range(2):
                fq = f[s, q]
                img[s, :, q * H:(q + 1) * H] = 2.0 * (fq[:, :H] * g[q][:, :H] + fq[:, H:] * g[q][:, H:])
            send1(ph, s)
            return 0

        lax.fori_loop(0, S, body, 0)

    halo_start(1, q0)
    images(1, q0)
    halo_end(1)
    laplace_to(q1, q0, halo.at[1], REG)
    ax[...] = jnp.zeros((2, 8, H), F32)
    sums(1)
    ax[0, 0:1, :] = dot_rows(whole(q0), whole(q0))
    ax[0, 1:2, :] = dot_rows(whole(q0), whole(q1))

    def keep_first(half, w):
        keep[half] = w
        ax[0, 2 + half:3 + half, :] = lanes((w * w).reshape(N * 8, B))
        return w

    sums_end(1, keep_first)
    give_back(1)
    adjoint(1, q1, 1)

    halo_start(2, q1)
    images(2, q1)
    ax[0, 4:5, :] = dot_rows(whole(q1), whole(q1))
    sum_start(0)
    halo_end(2)
    sums(2)
    sum_turn(0)
    red = sum_end(0)
    res, hah, aa = red[0:1], red[1:2] + red[2:3] + red[3:4], red[4:5]
    alpha = res / hah
    beta = (res - 2.0 * alpha * hah + alpha * alpha * aa) / res
    one = 1.0 + beta
    alpha_s, one_s = alpha[0, 0], one[0, 0]

    def second(half, w):
        w = one_s * keep[half] - alpha_s * w
        ax[1, 2 + half:3 + half, :] = lanes((w * w).reshape(N * 8, B))
        return w

    sums_end(2, second)
    for part in range(2):
        h2[part] = one_s * q0[part] - alpha_s * q1[part]
        q1[part] = q0[part] - alpha_s * q1[part]
    for i in range(4):
        halo[2, i] = one_s * halo[1, i] - alpha_s * halo[2, i]
    laplace_to(resid, h2, halo.at[2], REG)
    ax[1, 0:1, :] = dot_rows(whole(q1), whole(q1))
    ax[1, 1:2, :] = dot_rows(whole(h2), whole(resid))
    sum_start(1)
    give_back(2)
    sum_turn(1)
    adjoint(2, resid, 1)
    red = sum_end(1)
    alpha2 = (red[0:1] / (red[1:2] + red[2:3] + red[3:4]))[0, 0]
    for part in range(2):
        step[part] = alpha_s * q0[part] + alpha2 * h2[part]
        resid[part] = q1[part] - alpha2 * resid[part]


def routes(led_count, led_owner, led_offset):
    row = lax.axis_index("ty") * N
    column = lax.axis_index("tx")
    owner = lax.dynamic_slice_in_dim(led_owner, row, N, 0)
    count = lax.dynamic_slice_in_dim(led_count, row, N, 0)
    offset = lax.dynamic_slice_in_dim(led_offset, row, N, 0)
    slots = jnp.arange(S, dtype=jnp.int32)
    ids = jnp.arange(N, dtype=jnp.int32)
    live = slots[None, :] < count[:, None]
    hit = (owner[:, :, None] == ids[None, None, :]) & live[:, :, None]
    served = jnp.sum(hit.astype(jnp.int32), axis=1)
    rank = jnp.sum(served[None, :, :] * (ids[None, :, None] < ids[:, None, None]).astype(jnp.int32), axis=1)
    slot = jnp.where(served > 0, rank, S + 1).T
    chosen = (served[:, :, None] > 0) & (rank[:, :, None] == slots[None, None, :])
    cap = jnp.sum(jnp.where(chosen, ids[:, None, None], 0), axis=0)
    mine = lax.dynamic_slice_in_dim(chosen.astype(jnp.int32), column, 1, 1)[:, 0]
    own = lax.dynamic_slice_in_dim(hit.astype(jnp.int32), column, 1, 2)
    corner = jnp.sum(own * offset, axis=1)
    rc = jnp.sum(mine[:, :, None] * corner[:, None, :], axis=0)
    rc = jnp.concatenate([rc, jnp.sum(mine, axis=0)[:, None]], axis=1)
    return slot, cap, rc


def on_device(spectrum, measured, pupil_mask, led_count, led_owner, led_offset):
    highest = lax.Precision.HIGHEST
    slot, cap, rc = routes(led_count, led_owner, led_offset)
    pick = np.zeros((B, B), np.float32)
    for p in range(2):
        pick[p * H + np.arange(H), 2 * np.arange(H) + p] = 1.0
    pick = jnp.asarray(pick)
    meas = jnp.dot(jnp.dot(pick, measured[0], precision=highest), pick.T, precision=highest)
    dma = pltpu.SemaphoreType.DMA
    out = jax.ShapeDtypeStruct((2, T, T), F32)

    def vm(*shape):
        return pltpu.VMEM(shape, F32)

    return pl.pallas_call(
        kernel, out_shape=(out, out), in_specs=[SM, SM, SM, VM, VM, VM, VM], out_specs=(VM, VM),
        scratch_shapes=[
            vm(S, 2, B, B), vm(S, B, B), vm(S, B, B), vm(3, 2, 4, S + 2, 32, B), vm(2, N, 32, B),
            vm(3, 2, 4, N, 8, B), vm(3, 2, N, 32, B), vm(2, 3, S, 32, B), vm(3, S, B, B), vm(2, N, 8, B),
            vm(3, 4, 2, T), vm(3, 4, 2, T), vm(2, T, T), vm(2, T, T), vm(2, T, T),
            vm(2, 8, H), vm(2, 16, 8, H), vm(2, 8, 8, H), vm(2, 8, H),
            dma((3, 12)), dma((3, S)), dma((2, 4)),
        ],
        compiler_params=pltpu.CompilerParams(collective_id=0, has_side_effects=True, vmem_limit_bytes=63 << 20),
        name="update",
    )(slot, cap, rc, spectrum, pupil_mask, meas, tables())


def solution(mesh):
    placed = (P(None, "ty", "tx"), P(("ty", "tx"), None, None), P(), P(), P(), P())
    return jax.shard_map(
        on_device, mesh=mesh, in_specs=placed,
        out_specs=(P(None, "ty", "tx"), P(None, "ty", "tx")), check_vma=False)
```

time: 1160 us -> 161 us (0.14); the launches traced: 1150 us -> 160 us
  blocking collectives: 308 us -> 0 us
  matrix products: 263 us -> 3.39 us
  waiting for transfers between devices: 187 us -> 0 us
  local copies, waits for them, and re-layouts: 180 us -> 6.41 us
  Pallas kernels: 0 us -> 146 us
  other arithmetic: 112 us -> 3.48 us
  starting transfers between devices: 60.8 us -> 0 us
  between operations: 35.9 us -> 0.71 us
    dot_general x54 -> x2, matrix products: 263 us -> 3.39 us  [the longest x1 2.07 us: on_device(): jnp.dot(jnp.dot(pick, measured[0], precision=highest), pick.T, precision=...]
    psum x3 -> x0, blocking collectives: 201 us -> none  [the longest x2 136 us: squared(): return lax.psum(jnp.sum(values * values), ('ty', 'tx'))]
    dynamic_update_slice x24 -> x0, local copies, waits for them, and re-layouts: 150 us -> none  [adjoint(): lax.dynamic_update_slice(deposit, window + contrib[slot_no], corner)]
    pallas_call x0 -> x1, Pallas kernels: none -> 146 us  [on_device(): pl.pallas_call(kernel, out_shape=(out, out), in_specs=[SM, SM, SM, VM, VM...]
    ppermute x12 -> x0, waiting for transfers between devices: 118 us -> none  [the longest x6 115 us: extended(): after = lax.ppermute(initial, axis, down)]
    all_to_all x2 -> x0, blocking collectives: 107 us -> none  [to_capture(): lax.all_to_all(dest_term, 'tx', split_axis=0, concat_axis=0, tiled=True)]
    all_to_all x4 -> x0, waiting for transfers between devices: 69.8 us -> none  [the longest x1 62 us: to_capture(): lax.all_to_all(dest_term, 'tx', split_axis=0, concat_axis=0, tiled=True)]
    add x22 -> x0, other arithmetic: 50.9 us -> none  [the longest x21 48.2 us: adjoint(): window + contrib[slot_no]]
  transfers between devices with their start and end apart: 16 -> 0, of which waited for: 10 -> 0; matrix products, arithmetic and copies ran while one was open for 1% -> 0% of each run, Pallas kernels for 0% -> 0%
where the time goes in v2:
time: 161 us; the launch traced here: 160 us
  Pallas kernels  146 us (91%)
  local copies, waits for them, and re-layouts  6.41 us (4%)
  other arithmetic  3.48 us (2%)
  matrix products  3.39 us (2%)
    pallas_call x1, Pallas kernels, on_device(): pl.pallas_call(kernel, out_shape=(out, out), in_specs=[SM, SM, SM, VM, VM...  146 us
    unnamed x6, local copies, waits for them, and re-layouts  4.56 us

profile of v2, /device:TPU:1, one launch (start us, length us, event | category | flops | bytes accessed | tf_op | source)
XLA Modules:
  0.0 160.3 jit_solution(17189596025727864605)
XLA Ops:
  0.6 0.0 copy-start
  0.7 0.8 dynamic_slice.16
  1.4 0.8 constant_dynamic-slice_fusion
  2.2 0.1 copy.17
  2.3 0.1 multiply_reduce_fusion
  2.4 0.1 copy.18
  2.5 0.6 select_bitcast_fusion
  3.1 0.9 select_reduce_fusion.cap
  4.1 0.1 convert_reduce_fusion
  4.2 0.1 copy.21
  4.3 0.8 multiply_reduce_fusion.2
  5.1 0.1 multiply_reduce_fusion.1
  5.3 0.1 copy.20
  5.3 0.7 pad_add_fusion.rc
  6.0 0.0 copy-done
  6.0 1.3 fusion
  7.4 2.1 %fusion.7.meas = f32[256,256]{1,0:T(8,128)} fusion(f32[256,256]{1,0:T(8,128)S(1)} %fusion, f32[256,256]{1,0:T(8,128)} %constant.23.clone), kind=kOutput, calls=%fused_computation.22 | convolution fusion | flops 201326592 | bytes 786432 | tf_op jit(solution)/shard_map/dot_general | solution.py:430
  9.4 146.3 %update.1 = (f32[2,512,512]{2,1,0:T(8,128)}, f32[2,512,512]{2,1,0:T(8,128)}) custom-call(s32[16,16]{1,0:T(8,128)} %get-tuple-element.2.slot, s32[16,8]{1,0:T(8,128)} %select_reduce_fusion.cap, s32[8,3]{1,0:T(8,128)} %pad_add_fusion.rc, f32[2,512,512]{2,1,0:T(8,128)} %spectrum.1, s32[256,256]{1,0:T(8,128)} %mask.1, f32[256,256]{1,0:T(8,128)} %fusion.7.meas, ...), custom_call_target="tpu_custom_call" | custom-call | tf_op jit(solution)/shard_map/update/pallas_call | solution.py:437
  155.7 0.0 copy-start.1
  155.7 3.2 %copy.24 = f32[2,512,512]{2,1,0:T(8,128)} copy(f32[2,512,512]{2,1,0:T(8,128)} %get-tuple-element.6) | data formatting | bytes 4194304
  158.9 0.0 copy-done.1
  158.9 1.3 copy.25
  (7 shorter events, 0.1 us)
Async XLA Ops:
  0.6 5.4 %copy-start = (f32[1,256,256]{2,1,0:T(8,128)S(1)}, f32[1,256,256]{2,1,0:T(8,128)}, u32[]{:S(2)}) copy-start(f32[1,256,256]{2,1,0:T(8,128)} %param.9) | copy-start | bytes 786436
  155.7 3.2 %copy-start.1 = (f32[2,512,512]{2,1,0:T(8,128)S(1)}, f32[2,512,512]{2,1,0:T(8,128)}, u32[]{:S(2)}) copy-start(f32[2,512,512]{2,1,0:T(8,128)} %get-tuple-element.7) | copy-start | bytes 6291460

commit v3 on v2

v3 whole, which is shorter than its diff:
```python
import jax
import jax.numpy as jnp
import numpy as np
from jax import lax
from jax.experimental import pallas as pl
from jax.experimental.pallas import tpu as pltpu
from jax.sharding import PartitionSpec as P

B = 256
H = 128
T = 512
S = 8
N = 16
REG = 0.5
F32 = jnp.float32
BF = jnp.bfloat16
MESH = pl.DeviceIdType.MESH
LIMIT = 52 << 20
LAG = 2
LEAD = 3
VM = pl.BlockSpec(memory_space=pltpu.VMEM)


def tables():
    m = np.arange(H)
    out = []
    for p in range(2):
        ang = ((2 * m[:, None] + p) * m[None, :] % B) * (2.0 * np.pi / B)
        re, im = np.cos(ang) / 16.0, np.sin(ang) / 16.0
        out.append(np.block([[re, -im], [im, re]]))
    full = np.stack([out[0], out[1], out[0].T, out[1].T])
    hi = full.astype(np.float32).astype(jnp.bfloat16)
    lo = (full - hi.astype(np.float64)).astype(np.float32).astype(jnp.bfloat16)
    return jnp.asarray(np.stack([hi, lo]))


def split(x):
    hi = x.astype(BF)
    return hi, (x - hi.astype(F32)).astype(BF)


def mm(a, b):
    return jnp.dot(a, b, preferred_element_type=F32)


def left(tab, k, x):
    hi, lo = split(x)
    return mm(tab[0, k], hi) + (mm(tab[0, k], lo) + mm(tab[1, k], hi))


def right(tab, k, x):
    hi, lo = split(x)
    return mm(hi, tab[0, k]) + (mm(lo, tab[0, k]) + mm(hi, tab[1, k]))


def masks(r, c, rows, base):
    row = lax.broadcasted_iota(jnp.int32, (rows, B), 0) + base < r
    col = lax.broadcasted_iota(jnp.int32, (rows, B), 1) < c
    return row, col


def gather(v, part, s, r, c, pup):
    halves = []
    for k1 in range(2):
        a = k1 * H
        row, col = masks(r, c, H, a)
        top = jnp.where(col, v[part, a:a + H, B:T], v[part, a:a + H, 0:B])
        bot = jnp.where(col, v[part, B + a:B + a + H, B:T], v[part, B + a:B + a + H, 0:B])
        halves.append(jnp.where(row, bot, top) * pup[s, a:a + H, :])
    return halves


def forward(v, s, r, c, pup, tab):
    re, im = gather(v, 0, s, r, c, pup), gather(v, 1, s, r, c, pup)
    rows = []
    for p in range(2):
        if p == 0:
            a = jnp.concatenate([re[0] + re[1], im[0] + im[1]], axis=0)
        else:
            a = jnp.concatenate([re[0] - re[1], im[0] - im[1]], axis=0)
        rows.append(left(tab, p, a))
    out = []
    for q in range(2):
        b = []
        for p in range(2):
            y = rows[p]
            z = y[:, :H] + y[:, H:] if q == 0 else y[:, :H] - y[:, H:]
            b.append(jnp.concatenate([z[:H], z[H:]], axis=1))
        out.append(right(tab, 2 + q, jnp.concatenate(b, axis=0)))
    return out


def backward(f, s, w, tab):
    g = []
    for q in range(2):
        wq = w[q]
        g.append(right(tab, q, f[s, q] * jnp.concatenate([wq, wq], axis=1)))
    a, b = g[0] + g[1], g[0] - g[1]
    re = jnp.concatenate([a[:, :H], b[:, :H]], axis=1)
    im = jnp.concatenate([a[:, H:], b[:, H:]], axis=1)
    y = []
    for p in range(2):
        y.append(left(tab, 2 + p, jnp.concatenate([re[p * H:(p + 1) * H], im[p * H:(p + 1) * H]], axis=0)))
    plus, minus = y[0] + y[1], y[0] - y[1]
    return (plus[:H], minus[:H]), (plus[H:], minus[H:])


def deposit(out, s, r, c, pup, parts):
    for k1 in range(2):
        a = k1 * H
        row, col = masks(r, c, H, a)
        pu = pup[s, a:a + H, :]
        for part in range(2):
            x = parts[part][k1] * pu
            up, down = jnp.where(row, 0.0, x), jnp.where(row, x, 0.0)
            out[part, a:a + H, 0:B] += jnp.where(col, 0.0, up)
            out[part, a:a + H, B:T] += jnp.where(col, up, 0.0)
            out[part, B + a:B + a + H, 0:B] += jnp.where(col, 0.0, down)
            out[part, B + a:B + a + H, B:T] += jnp.where(col, down, 0.0)


def pack_edges(v, edge):
    for part in range(2):
        edge[0, part:part + 1, :] = v[part, 0:1, :]
        edge[1, part:part + 1, :] = v[part, T - 1:T, :]
        edge[2, part:part + 1, :] = jnp.transpose(v[part, :, 0:H])[0:1, :]
        edge[3, part:part + 1, :] = jnp.transpose(v[part, :, T - H:T])[H - 1:H, :]


def laplace_to(out, v, halo, scale):
    row = lax.broadcasted_iota(jnp.int32, (T, T), 0)
    col = lax.broadcasted_iota(jnp.int32, (T, T), 1)
    lcol, rcol = jnp.transpose(halo[2]), jnp.transpose(halo[3])
    for part in range(2):
        x = v[part]
        up = jnp.where(row == 0, halo[0, part:part + 1, :], pltpu.roll(x, 1, axis=0))
        down = jnp.where(row == T - 1, halo[1, part:part + 1, :], pltpu.roll(x, T - 1, axis=0))
        lt = jnp.where(col == 0, lcol[:, part:part + 1], pltpu.roll(x, 1, axis=1))
        rt = jnp.where(col == T - 1, rcol[:, part:part + 1], pltpu.roll(x, T - 1, axis=1))
        out[part] = scale * (4.0 * x - ((up + down) + (lt + rt)))


def lanes(x):
    one = jnp.sum(x, axis=0, keepdims=True)
    acc = one[:, 0:H]
    for i in range(H, x.shape[1], H):
        acc = acc + one[:, i:i + H]
    return acc


def dot_rows(a, b):
    acc = jnp.zeros((1, H), F32)
    for part in range(2):
        acc = acc + lanes(a(part) * b(part))
    return acc


def whole(ref):
    return lambda part: ref[part]


def prefix(x, lane):
    total = x
    for k in (1, 2, 4, 8):
        total = total + jnp.where(lane >= k, pltpu.roll(total, k, axis=1), 0)
    return total - x


def route(ty, tx, count, owner, offset, table):
    lane = lax.broadcasted_iota(jnp.int32, (N, H), 1)
    cap_id = lane - ty * N
    group = (cap_id >= 0) & (cap_id < N)
    live = lax.broadcasted_iota(jnp.int32, (S, H), 0) < count[...]
    rows = []
    for a in range(N):
        rows.append(jnp.max(jnp.where((owner[...] == a) & live, 1, 0), axis=0, keepdims=True))
    served = jnp.where(group, jnp.concatenate(rows, axis=0), 0)
    rank = prefix(served, jnp.bitwise_and(lane, N - 1))
    table[0:N] = jnp.where(served > 0, rank, S + 1)
    caps = jnp.zeros((N, H), jnp.int32)
    for k in range(S):
        at = jnp.sum(jnp.where((served > 0) & (rank == k), cap_id, 0), axis=1, keepdims=True)
        caps = jnp.where(lane == k, at, caps)
    table[N:2 * N] = caps
    hit = jnp.where((owner[...] == tx) & live, 1, 0)
    mine = lax.broadcasted_iota(jnp.int32, (N, H), 0) == tx
    own = jnp.sum(jnp.where(mine, served, 0), axis=0, keepdims=True)
    order = jnp.sum(jnp.where(mine, rank, 0), axis=0, keepdims=True)
    slot_id = lax.broadcasted_iota(jnp.int32, (S, H), 0)
    chosen = jnp.where((own > 0) & (order == slot_id), 1, 0)
    lane8 = lax.broadcasted_iota(jnp.int32, (S, H), 1)
    out = jnp.where(lane8 == 2, jnp.sum(chosen, axis=1, keepdims=True), 0)
    for k in range(2):
        corner = jnp.zeros((1, H), jnp.int32)
        for t in range(S):
            corner = corner + hit[t:t + 1] * offset[t, k:k + 1, :]
        out = jnp.where(lane8 == k, jnp.sum(chosen * corner, axis=1, keepdims=True), out)
    table[2 * N:2 * N + S] = out


def reorder(x, pick):
    def terms(v):
        hi, rest = split(v)
        rest = v - hi.astype(F32)
        mid, low = split(rest)
        return hi, mid, low

    p, pt = pick[0], pick[1]
    a, b, c = terms(x)
    y = mm(p, a) + (mm(p, b) + mm(p, c))
    a, b, c = terms(y)
    return mm(a, pt) + (mm(b, pt) + mm(c, pt))


def kernel(count, owner, offset, spectrum, mask, measured, tab, pick, step, resid,
           f, pup, img, r1a, r1b, p2, r2, wla, wlb, sb, wret, keep, edge, halo, q0, q1, h2, meas, table, tabs, ax, arx, ary, amid,
           sem, sem4, asem, lsem):
    tx, ty = lax.axis_index("tx"), lax.axis_index("ty")
    z, y = tx // 4, tx % 4
    zd = [z] + [lax.rem(z + d, 4) for d in range(1, 4)]
    yd = [y] + [lax.rem(y + d, 4) for d in range(1, 4)]
    tile = [[zd[d] * 4 + y for d in range(4)], [z * 4 + yd[d] for d in range(4)]]
    across, along, atile = [zd, yd], [yd, zd], [tile[1], tile[0]]
    r1, wl = (r1a, r1b), (wla, wlb)
    tx_dev = [{"tx": lax.rem(tx + d, 16)} for d in range(16)]
    ty_dev = [{"ty": lax.rem(ty + d, 8)} for d in range(8)]
    edge_dev = [ty_dev[7], ty_dev[1], tx_dev[15], tx_dev[1]]

    def remote(src, dst, send, recv, dev):
        return pltpu.make_async_remote_copy(
            src_ref=src, dst_ref=dst, send_sem=send, recv_sem=recv, device_id=dev, device_id_type=MESH)

    def wait_sent(ref, s):
        remote(ref, ref, s, s, tx_dev[1]).wait_send()

    def wait_got(ref, s):
        remote(ref, ref, s, s, tx_dev[1]).wait_recv()

    def al(x, k):
        return pl.multiple_of(x * k, 8)

    def line_rows(half, d):
        return pl.ds(half * H + al(across[half][d], 32), 32)

    def sum_start(k):
        for d in range(1, 16):
            remote(ax.at[k], arx.at[k, d], asem.at[k, 0], asem.at[k, 1], tx_dev[d]).start()

    def sum_turn(k):
        wait_sent(arx.at[k, 1:16], asem.at[k, 0])
        wait_got(arx.at[k, 1:16], asem.at[k, 1])
        acc = ax[k]
        for d in range(1, 16):
            acc = acc + arx[k, d]
        amid[k] = acc
        for d in range(1, 8):
            remote(amid.at[k], ary.at[k, d], asem.at[k, 2], asem.at[k, 3], ty_dev[d]).start()

    def sum_end(k):
        wait_sent(ary.at[k, 1:8], asem.at[k, 2])
        wait_got(ary.at[k, 1:8], asem.at[k, 3])
        acc = amid[k]
        for d in range(1, 8):
            acc = acc + ary[k, d]
        return jnp.sum(acc, axis=1, keepdims=True)

    def halo_start(ph, v):
        pack_edges(v, edge.at[ph])
        for i, dst in enumerate((1, 0, 3, 2)):
            remote(edge.at[ph, i], halo.at[ph, dst], sem.at[ph, 0, 0], sem.at[ph, 0, 1], edge_dev[i]).start()

    def halo_end(ph):
        wait_sent(edge.at[ph], sem.at[ph, 0, 0])
        wait_got(halo.at[ph], sem.at[ph, 0, 1])
        for i, inside in enumerate((ty > 0, ty < 7, tx > 0, tx < 15)):
            halo[ph, i] = jnp.where(inside, halo[ph, i], 0.0)

    def send1(ph, q, s):
        for d in (2, 1, 3):
            for half in range(2):
                remote(img.at[q, s, line_rows(half, d), :], r1[q].at[ph, half, 4 - d, s],
                       sem.at[ph, q, 2], sem.at[ph, q, 3], {"tx": tile[half][d]}).start()
        for half in range(2):
            r1[q][ph, half, 0, s] = img[q, s, line_rows(half, 0), :]

    def send_meas():
        for q in range(2):
            for d in (2, 1, 3):
                for half in range(2):
                    remote(meas.at[q, line_rows(half, d), :], r1[q].at[0, half, 4 - d, S],
                           sem.at[0, q, 10], sem.at[0, q, 11], {"tx": tile[half][d]}).start()
            for half in range(2):
                r1[q][0, half, 0, S] = meas[q, line_rows(half, 0), :]

    def transforms(ph, low, high, image):
        def body(s, _):
            image(s)
            send1(ph, 0, s)

            @pl.when(s >= LAG)
            def _():
                send1(ph, 1, s - LAG)

            return 0

        lax.fori_loop(low, high, body, 0)
        if high == S:
            for s in range(S - LAG, S):
                send1(ph, 1, s)

    def sums(ph, q):
        wait_sent(img.at[q, 0:6], sem.at[ph, q, 2])
        wait_got(r1[q].at[ph, :, 1:4, 0:S], sem.at[ph, q, 3])
        if ph == 0:
            wait_sent(r1[q].at[ph, :, 1:4, S], sem.at[ph, q, 10])
            wait_got(r1[q].at[ph, :, 1:4, S], sem.at[ph, q, 11])

        def partial(c, _):
            for half in range(2):
                acc = r1[q][ph, half, 0, slot_at(tile[half][0], c)]
                for d in range(1, 4):
                    acc = acc + r1[q][ph, half, d, slot_at(tile[half][d], c)]
                p2[q, half, c] = acc
            return 0

        lax.fori_loop(0, N, partial, 0, unroll=4)
        if ph == 0:
            for half in range(2):
                for d in range(4):
                    p2[q, half, tile[half][d]] -= r1[q][ph, half, d, S]
        for d in (2, 1, 3):
            for half in range(2):
                remote(p2.at[q, half, :, pl.ds(al(along[half][d], 8), 8), :], r2.at[ph, q, half, 4 - d],
                       sem.at[ph, q, 4], sem.at[ph, q, 5], {"tx": atile[half][d]}).start()

    def mine(half):
        return pl.ds(al(along[half][0], 8), 8)

    def sums_end(ph, q, fix):
        wait_sent(r2.at[ph, q, :, 1:4], sem.at[ph, q, 4])
        wait_got(r2.at[ph, q, :, 1:4], sem.at[ph, q, 5])
        for half in range(2):
            w = (p2[q, half, :, mine(half), :] + r2[ph, q, half, 1]) + (r2[ph, q, half, 2] + r2[ph, q, half, 3])
            wl[q][ph, half, :, mine(half), :] = fix(q, half, w)
        for d in (2, 1, 3):
            for half in range(2):
                part = wl[q].at[ph, half, :, mine(half), :]
                remote(part, part, sem.at[ph, q, 6], sem.at[ph, q, 7], {"tx": atile[half][d]}).start()

    def got3(ph, q):
        wait_sent(wl[q].at[ph, :, :, 0:24, :], sem.at[ph, q, 6])
        wait_got(wl[q].at[ph, :, :, 0:24, :], sem.at[ph, q, 7])

    def send4(ph, q, s):
        for d in (2, 1, 3):
            for half in range(2):
                sb[q, half, d - 1, s] = wl[q][ph, half, cap_at(tile[half][d], s)]
                remote(sb.at[q, half, d - 1, s], wret.at[ph, s, q, line_rows(half, 0), :],
                       sem.at[ph, 0, 8], sem4.at[ph, s], {"tx": tile[half][d]}).start()
        for half in range(2):
            wret[ph, s, q, line_rows(half, 0), :] = wl[q][ph, half, cap_at(tile[half][0], s)]

    def give_back(ph, between=None):
        got3(ph, 0)
        lax.fori_loop(0, LEAD, lambda s, _: (send4(ph, 0, s), 0)[1], 0)
        if between is not None:
            between()
        got3(ph, 1)
        lax.fori_loop(0, LEAD, lambda s, _: (send4(ph, 1, s), 0)[1], 0)

        def rest(s, _):
            send4(ph, 0, s)
            send4(ph, 1, s)
            return 0

        lax.fori_loop(LEAD, S, rest, 0)

    def adjoint(ph, out, sign):
        def body(s, _):
            wait_got(wret.at[ph, s, :, 0:192, :], sem4.at[ph, s])
            w = [wret[ph, s, q] * (2.0 * sign) for q in range(2)]
            r, c = corner(s)
            deposit(out, s, r, c, pup, backward(f, s, w, tab))
            return 0

        lax.fori_loop(0, S, body, 0)
        wait_sent(sb, sem.at[ph, 0, 8])

    def slot_at(a, c):
        return tabs[a, ty * N + c]

    def cap_at(a, s):
        return tabs[N + a, s]

    def corner(s):
        return tabs[2 * N + s, 0], tabs[2 * N + s, 1]

    bar = pltpu.get_barrier_semaphore()
    for dev in tx_dev[1:] + ty_dev[1:]:
        pl.semaphore_signal(bar, inc=1, device_id=dev, device_id_type=MESH)
    for ph in range(3):
        for half in range(2):
            for d in range(4):
                for q in range(2):
                    r1[q][ph, half, d, S + 1] = jnp.zeros((32, H), F32)
    route(ty, tx, count, owner, offset, table)
    to_scalar = pltpu.make_async_copy(table, tabs, lsem)
    to_scalar.start()
    ordered = reorder(measured[0], pick)
    for q in range(2):
        meas[q] = ordered[:, q * H:(q + 1) * H]
    ax[...] = jnp.zeros((2, 8, H), F32)
    to_scalar.wait()
    pl.semaphore_wait(bar, 22)

    send_meas()

    def fields(s):
        r, c = corner(s)
        base = mask[...].astype(F32)
        rolled = pltpu.roll(pltpu.roll(base, jnp.bitwise_and(r, B - 1), axis=0), jnp.bitwise_and(c, B - 1), axis=1)
        pup[s] = rolled * tabs[2 * N + s, 2].astype(F32)
        g = forward(spectrum, s, r, c, pup, tab)
        for q in range(2):
            f[s, q] = g[q]
            img[q, s] = g[q][:, :H] * g[q][:, :H] + g[q][:, H:] * g[q][:, H:]

    def image_of(v):
        def image(s):
            r, c = corner(s)
            g = forward(v, s, r, c, pup, tab)
            for q in range(2):
                fq = f[s, q]
                img[q, s] = 2.0 * (fq[:, :H] * g[q][:, :H] + fq[:, H:] * g[q][:, H:])

        return image

    transforms(0, 0, S, fields)
    halo_start(0, spectrum)
    sums(0, 0)
    sums(0, 1)
    halo_end(0)
    laplace_to(q0, spectrum, halo.at[0], -REG)
    for q in range(2):
        sums_end(0, q, lambda q, half, w: w)
    give_back(0)
    adjoint(0, q0, -1.0)

    transforms(1, 0, S, image_of(q0))
    halo_start(1, q0)
    sums(1, 0)
    sums(1, 1)
    halo_end(1)
    laplace_to(q1, q0, halo.at[1], REG)

    def keep_first(q, half, w):
        keep[q, half] = w
        k = 2 + 2 * q + half
        ax[0, k:k + 1, :] = lanes((w * w).reshape(N * 8, H))
        return w

    for q in range(2):
        sums_end(1, q, keep_first)
    ax[0, 0:1, :] = dot_rows(whole(q0), whole(q0))
    ax[0, 1:2, :] = dot_rows(whole(q0), whole(q1))
    give_back(1)
    adjoint(1, q1, 1.0)

    transforms(2, 0, 2, image_of(q1))
    ax[0, 6:7, :] = dot_rows(whole(q1), whole(q1))
    sum_start(0)
    transforms(2, 2, S, image_of(q1))
    halo_start(2, q1)
    sum_turn(0)
    sums(2, 0)
    sums(2, 1)
    red = sum_end(0)

    def heading_image(red):
        return (red[1:2] + red[2:3]) + ((red[3:4] + red[4:5]) + red[5:6])

    res, hah, aa = red[0:1], heading_image(red), red[6:7]
    alpha = res / hah
    beta = (res - 2.0 * alpha * hah + alpha * alpha * aa) / res
    alpha_s, one_s = alpha[0, 0], (1.0 + beta)[0, 0]
    halo_end(2)
    for i in range(4):
        halo[2, i] = one_s * halo[1, i] - alpha_s * halo[2, i]
    for part in range(2):
        h2[part] = one_s * q0[part] - alpha_s * q1[part]
        q1[part] = q0[part] - alpha_s * q1[part]
    laplace_to(resid, h2, halo.at[2], REG)

    def second(q, half, w):
        w = one_s * keep[q, half] - alpha_s * w
        k = 2 + 2 * q + half
        ax[1, k:k + 1, :] = lanes((w * w).reshape(N * 8, H))
        return w

    for q in range(2):
        sums_end(2, q, second)
    ax[1, 0:1, :] = dot_rows(whole(q1), whole(q1))
    ax[1, 1:2, :] = dot_rows(whole(h2), whole(resid))
    sum_start(1)
    give_back(2, lambda: sum_turn(1))
    red = sum_end(1)
    alpha2 = (red[0:1] / heading_image(red))[0, 0]
    for part in range(2):
        step[part] = alpha_s * q0[part] + alpha2 * h2[part]
        resid[part] = q1[part] - alpha2 * resid[part]
    adjoint(2, resid, -alpha2)


def on_device(spectrum, measured, pupil_mask, led_count, led_owner, led_offset):
    pick = np.zeros((B, B), np.float32)
    for p in range(2):
        pick[p * H + np.arange(H), 2 * np.arange(H) + p] = 1.0
    pick = jnp.asarray(np.stack([pick, pick.T]).astype(jnp.bfloat16))
    dma = pltpu.SemaphoreType.DMA
    out = pltpu.VMEM((2, T, T), F32)

    def vm(*shape):
        return pltpu.VMEM(shape, F32)

    return pl.pallas_call(
        kernel, out_shape=(out, out), in_specs=[VM] * 8, out_specs=(VM, VM),
        scratch_shapes=[
            vm(S, 2, B, B), vm(S, B, B), vm(2, S, B, H), vm(3, 2, 4, S + 2, 32, H), vm(3, 2, 4, S + 2, 32, H), vm(2, 2, N, 32, H),
            vm(3, 2, 2, 4, N, 8, H), vm(3, 2, N, 32, H), vm(3, 2, N, 32, H), vm(2, 2, 3, S, 32, H), vm(3, S, 2, B, H),
            vm(2, 2, N, 8, H), vm(3, 4, 2, T), vm(3, 4, 2, T), vm(2, T, T), vm(2, T, T), vm(2, T, T), vm(2, B, H),
            pltpu.VMEM((40, H), jnp.int32), pltpu.SMEM((40, H), jnp.int32),
            vm(2, 8, H), vm(2, 16, 8, H), vm(2, 8, 8, H), vm(2, 8, H),
            dma((3, 2, 12)), dma((3, S)), dma((2, 4)), dma(()),
        ],
        compiler_params=pltpu.CompilerParams(collective_id=0, has_side_effects=True, vmem_limit_bytes=LIMIT),
        name="update",
    )(led_count.reshape(1, -1), led_owner.T, led_offset.transpose(1, 2, 0), spectrum, pupil_mask, measured,
      tables(), pick)


def solution(mesh):
    placed = (P(None, "ty", "tx"), P(("ty", "tx"), None, None), P(), P(), P(), P())
    return jax.shard_map(
        on_device, mesh=mesh, in_specs=placed,
        out_specs=(P(None, "ty", "tx"), P(None, "ty", "tx")), check_vma=False)
```

time: 161 us -> 136 us (0.84)
  Pallas kernels: 146 us -> 133 us
  local copies, waits for them, and re-layouts: 6.41 us -> 2.64 us
  other arithmetic: 3.48 us -> 0 us
  matrix products: 3.39 us -> 0 us
    pallas_call x1, Pallas kernels: 146 us -> 133 us  [on_device(): pl.pallas_call(kernel, out_shape=(out, out), in_specs=[VM] * 8, out_specs...]
    dot_general x2 -> x0, matrix products: 3.39 us -> none  [the longest x1 2.07 us: on_device(): jnp.dot(jnp.dot(pick, measured[0], precision=highest), pick.T, precision=...]
    reduce_sum x6 -> x0, other arithmetic: 2.15 us -> none  [the longest x1 0.95 us: routes(): cap = jnp.sum(jnp.where(chosen, ids[:, None, None], 0), axis=0)]
    unnamed x6 -> x2, local copies, waits for them, and re-layouts: 4.56 us -> 2.64 us
where the time goes in v3:
time: 136 us
  Pallas kernels  133 us (98%)
  local copies, waits for them, and re-layouts  2.64 us (2%)
    pallas_call x1, Pallas kernels, on_device(): pl.pallas_call(kernel, out_shape=(out, out), in_specs=[VM] * 8, out_specs...  133 us

profile of v3, /device:TPU:1, one launch (start us, length us, event | category | flops | bytes accessed | tf_op | source)
XLA Modules:
  0.0 135.9 jit_solution(2521267016904487502)
XLA Ops:
  0.6 132.7 %update.1 = (f32[2,512,512]{2,1,0:T(8,128)S(1)}, f32[2,512,512]{2,1,0:T(8,128)S(1)}) custom-call(s32[1,128]{1,0:T(1,128)} %bitcast.5, s32[8,128]{1,0:T(8,128)} %bitcast.4, s32[8,2,128]{2,1,0:T(2,128)} %bitcast.3, f32[2,512,512]{2,1,0:T(8,128)} %spectrum.1, s32[256,256]{1,0:T(8,128)} %mask.1, f32[1,256,256]{2,1,0:T(8,128)} %measured.1, ...), custom_call_target="tpu_custom_call" | custom-call | tf_op jit(solution)/shard_map/update/pallas_call | solution.py:525
  133.3 1.3 copy.12
  134.6 1.3 copy.13

commit v4 on v3

--- a/solution.py
+++ b/solution.py
@@ -16,9 +16,11 @@
 BF = jnp.bfloat16
 MESH = pl.DeviceIdType.MESH
 LIMIT = 52 << 20
-LAG = 2
-LEAD = 3
+ORDER = (1, 3, 2)
+CUT = 4
+GROUPS = ((0, 2), (2, 4), (4, 6), (6, 7), (7, 8))
 VM = pl.BlockSpec(memory_space=pltpu.VMEM)
+ANY = pl.BlockSpec(memory_space=pl.ANY)
 
 
 def tables():
@@ -212,8 +214,8 @@
     return mm(a, pt) + (mm(b, pt) + mm(c, pt))
 
 
-def kernel(count, owner, offset, spectrum, mask, measured, tab, pick, step, resid,
-           f, pup, img, r1a, r1b, p2, r2, wla, wlb, sb, wret, keep, edge, halo, q0, q1, h2, meas, table, tabs, ax, arx, ary, amid,
+def kernel(count, owner, offset, given, mask, measured, tab_in, pick, step, resid,
+           f, pup, img, r1a, r1b, p2, r2, wla, wlb, sb, wret, keep, edge, halo, q0, q1, h2, meas, back, spectrum, tab, last, table, tabs, ax, arx, ary, amid,
            sem, sem4, asem, lsem):
     tx, ty = lax.axis_index("tx"), lax.axis_index("ty")
     z, y = tx // 4, tx % 4
@@ -275,38 +277,48 @@
         for i, inside in enumerate((ty > 0, ty < 7, tx > 0, tx < 15)):
             halo[ph, i] = jnp.where(inside, halo[ph, i], 0.0)
 
-    def send1(ph, q, s):
-        for d in (2, 1, 3):
-            for half in range(2):
-                remote(img.at[q, s, line_rows(half, d), :], r1[q].at[ph, half, 4 - d, s],
-                       sem.at[ph, q, 2], sem.at[ph, q, 3], {"tx": tile[half][d]}).start()
-        for half in range(2):
-            r1[q][ph, half, 0, s] = img[q, s, line_rows(half, 0), :]
+    def send1(ph, q, low, count):
+        if count == 1:
+            src, dst = lambda rows: img.at[q, low, rows, :], lambda half, d: r1[q].at[ph, half, 4 - d, low]
+        else:
+            part = pl.ds(low, count)
+            src, dst = lambda rows: img.at[q, part, rows, :], lambda half, d: r1[q].at[ph, half, 4 - d, part]
+        for d in ORDER:
+            for half in range(2):
+                remote(src(line_rows(half, d)), dst(half, d), sem.at[ph, q, 2], sem.at[ph, q, 3],
+                       {"tx": tile[half][d]}).start()
+
+    def keep_own(ph, s):
+        for q in range(2):
+            for half in range(2):
+                r1[q][ph, half, 0, s] = img[q, s, line_rows(half, 0), :]
 
     def send_meas():
         for q in range(2):
-            for d in (2, 1, 3):
+            for d in ORDER:
                 for half in range(2):
                     remote(meas.at[q, line_rows(half, d), :], r1[q].at[0, half, 4 - d, S],
                            sem.at[0, q, 10], sem.at[0, q, 11], {"tx": tile[half][d]}).start()
             for half in range(2):
                 r1[q][0, half, 0, S] = meas[q, line_rows(half, 0), :]
 
-    def transforms(ph, low, high, image):
+    def transforms(ph, low, high, image, turn=None):
         def body(s, _):
             image(s)
-            send1(ph, 0, s)
-
-            @pl.when(s >= LAG)
+            send1(ph, 0, s, 1)
+
+            @pl.when(s == CUT - 1)
             def _():
-                send1(ph, 1, s - LAG)
-
+                send1(ph, 1, 0, CUT)
+
+            keep_own(ph, s)
+            if turn is not None:
+                pl.when(s == 5)(turn)
             return 0
 
         lax.fori_loop(low, high, body, 0)
         if high == S:
-            for s in range(S - LAG, S):
-                send1(ph, 1, s)
+            send1(ph, 1, CUT, S - CUT)
 
     def sums(ph, q):
         wait_sent(img.at[q, 0:6], sem.at[ph, q, 2])
@@ -320,70 +332,92 @@
                 acc = r1[q][ph, half, 0, slot_at(tile[half][0], c)]
                 for d in range(1, 4):
                     acc = acc + r1[q][ph, half, d, slot_at(tile[half][d], c)]
-                p2[q, half, c] = acc
+                p2[q, half, :, c] = acc.reshape(4, 8, H)
             return 0
 
         lax.fori_loop(0, N, partial, 0, unroll=4)
         if ph == 0:
             for half in range(2):
                 for d in range(4):
-                    p2[q, half, tile[half][d]] -= r1[q][ph, half, d, S]
-        for d in (2, 1, 3):
-            for half in range(2):
-                remote(p2.at[q, half, :, pl.ds(al(along[half][d], 8), 8), :], r2.at[ph, q, half, 4 - d],
+                    p2[q, half, :, tile[half][d]] -= r1[q][ph, half, d, S].reshape(4, 8, H)
+        for d in ORDER:
+            for half in range(2):
+                remote(p2.at[q, half, along[half][d]], r2.at[ph, q, half, 4 - d],
                        sem.at[ph, q, 4], sem.at[ph, q, 5], {"tx": atile[half][d]}).start()
-
-    def mine(half):
-        return pl.ds(al(along[half][0], 8), 8)
 
     def sums_end(ph, q, fix):
         wait_sent(r2.at[ph, q, :, 1:4], sem.at[ph, q, 4])
         wait_got(r2.at[ph, q, :, 1:4], sem.at[ph, q, 5])
         for half in range(2):
-            w = (p2[q, half, :, mine(half), :] + r2[ph, q, half, 1]) + (r2[ph, q, half, 2] + r2[ph, q, half, 3])
-            wl[q][ph, half, :, mine(half), :] = fix(q, half, w)
-        for d in (2, 1, 3):
-            for half in range(2):
-                part = wl[q].at[ph, half, :, mine(half), :]
+            w = (p2[q, half, along[half][0]] + r2[ph, q, half, 1]) + (r2[ph, q, half, 2] + r2[ph, q, half, 3])
+            wl[q][ph, half, along[half][0]] = fix(q, half, w)
+        for d in ORDER:
+            for half in range(2):
+                part = wl[q].at[ph, half, along[half][0]]
                 remote(part, part, sem.at[ph, q, 6], sem.at[ph, q, 7], {"tx": atile[half][d]}).start()
 
     def got3(ph, q):
-        wait_sent(wl[q].at[ph, :, :, 0:24, :], sem.at[ph, q, 6])
-        wait_got(wl[q].at[ph, :, :, 0:24, :], sem.at[ph, q, 7])
-
-    def send4(ph, q, s):
-        for d in (2, 1, 3):
-            for half in range(2):
-                sb[q, half, d - 1, s] = wl[q][ph, half, cap_at(tile[half][d], s)]
-                remote(sb.at[q, half, d - 1, s], wret.at[ph, s, q, line_rows(half, 0), :],
-                       sem.at[ph, 0, 8], sem4.at[ph, s], {"tx": tile[half][d]}).start()
-        for half in range(2):
-            wret[ph, s, q, line_rows(half, 0), :] = wl[q][ph, half, cap_at(tile[half][0], s)]
-
-    def give_back(ph, between=None):
+        wait_sent(wl[q].at[ph, :, 0:3], sem.at[ph, q, 6])
+        wait_got(wl[q].at[ph, :, 0:3], sem.at[ph, q, 7])
+
+    def stage4(ph, q, low, high):
+        for s in range(low, high):
+            for half in range(2):
+                for d in range(4):
+                    piece = wl[q][ph, half, :, cap_at(tile[half][d], s)].reshape(32, H)
+                    if d == 0:
+                        wret[ph, s, q, line_rows(half, 0), :] = piece
+                    else:
+                        sb[half, d - 1, s, q] = piece
+
+    def send4(ph, q, g):
+        low, high = GROUPS[g]
+        for d in ORDER:
+            for half in range(2):
+                if q is None:
+                    src, dst = sb.at[half, d - 1, low:high], wret.at[ph, low:high, :, line_rows(half, 0), :]
+                else:
+                    src, dst = sb.at[half, d - 1, low:high, q], wret.at[ph, low:high, q, line_rows(half, 0), :]
+                remote(src, dst, sem.at[ph, 0, 8], sem4.at[ph, g], {"tx": tile[half][d]}).start()
+
+    def give_back(ph):
         got3(ph, 0)
-        lax.fori_loop(0, LEAD, lambda s, _: (send4(ph, 0, s), 0)[1], 0)
-        if between is not None:
-            between()
+        stage4(ph, 0, *GROUPS[0])
+        send4(ph, 0, 0)
         got3(ph, 1)
-        lax.fori_loop(0, LEAD, lambda s, _: (send4(ph, 1, s), 0)[1], 0)
-
-        def rest(s, _):
-            send4(ph, 0, s)
-            send4(ph, 1, s)
+        stage4(ph, 1, *GROUPS[0])
+        send4(ph, 1, 0)
+        for g in range(1, len(GROUPS)):
+            for q in range(2):
+                stage4(ph, q, *GROUPS[g])
+            send4(ph, None, g)
+
+    def adjoint(ph, out, sign, late=None):
+        back[1] = jnp.zeros((2, B, B), F32)
+
+        def add_in(s, which):
+            r, c = corner(s)
+            deposit(out, s, r, c, pup, [[back[which, part, k * H:(k + 1) * H, :] for k in range(2)] for part in range(2)])
+
+        def body(s, _):
+            for g, (low, high) in enumerate(GROUPS):
+                @pl.when(s == low)
+                def _():
+                    wait_got(wret.at[ph, low:high, :, 0:192, :], sem4.at[ph, g])
+
+            if late is not None:
+                pl.when(s == 5)(late)
+            odd = lax.rem(s, 2)
+            add_in(jnp.maximum(s - 1, 0), 1 - odd)
+            w = [wret[ph, s, q] * (2.0 * sign) for q in range(2)]
+            parts = backward(f, s, w, tab)
+            for part in range(2):
+                for k in range(2):
+                    back[odd, part, k * H:(k + 1) * H, :] = parts[part][k]
             return 0
 
-        lax.fori_loop(LEAD, S, rest, 0)
-
-    def adjoint(ph, out, sign):
-        def body(s, _):
-            wait_got(wret.at[ph, s, :, 0:192, :], sem4.at[ph, s])
-            w = [wret[ph, s, q] * (2.0 * sign) for q in range(2)]
-            r, c = corner(s)
-            deposit(out, s, r, c, pup, backward(f, s, w, tab))
-            return 0
-
         lax.fori_loop(0, S, body, 0)
+        add_in(S - 1, (S - 1) % 2)
         wait_sent(sb, sem.at[ph, 0, 8])
 
     def slot_at(a, c):
@@ -398,22 +432,23 @@
     bar = pltpu.get_barrier_semaphore()
     for dev in tx_dev[1:] + ty_dev[1:]:
         pl.semaphore_signal(bar, inc=1, device_id=dev, device_id_type=MESH)
+    loads = [pltpu.make_async_copy(given, spectrum, lsem.at[1]), pltpu.make_async_copy(tab_in, tab, lsem.at[2])]
+    for copy in loads:
+        copy.start()
     for ph in range(3):
         for half in range(2):
             for d in range(4):
                 for q in range(2):
                     r1[q][ph, half, d, S + 1] = jnp.zeros((32, H), F32)
     route(ty, tx, count, owner, offset, table)
-    to_scalar = pltpu.make_async_copy(table, tabs, lsem)
+    to_scalar = pltpu.make_async_copy(table, tabs, lsem.at[0])
     to_scalar.start()
     ordered = reorder(measured[0], pick)
     for q in range(2):
         meas[q] = ordered[:, q * H:(q + 1) * H]
     ax[...] = jnp.zeros((2, 8, H), F32)
-    to_scalar.wait()
-    pl.semaphore_wait(bar, 22)
-
-    send_meas()
+    for copy in [to_scalar] + loads:
+        copy.wait()
 
     def fields(s):
         r, c = corner(s)
@@ -435,7 +470,12 @@
 
         return image
 
-    transforms(0, 0, S, fields)
+    fields(0)
+    pl.semaphore_wait(bar, 22)
+    send_meas()
+    send1(0, 0, 0, 1)
+    keep_own(0, 0)
+    transforms(0, 1, S, fields)
     halo_start(0, spectrum)
     sums(0, 0)
     sums(0, 1)
@@ -469,9 +509,8 @@
     transforms(2, 0, 2, image_of(q1))
     ax[0, 6:7, :] = dot_rows(whole(q1), whole(q1))
     sum_start(0)
-    transforms(2, 2, S, image_of(q1))
+    transforms(2, 2, S, image_of(q1), lambda: sum_turn(0))
     halo_start(2, q1)
-    sum_turn(0)
     sums(2, 0)
     sums(2, 1)
     red = sum_end(0)
@@ -502,13 +541,21 @@
     ax[1, 0:1, :] = dot_rows(whole(q1), whole(q1))
     ax[1, 1:2, :] = dot_rows(whole(h2), whole(resid))
     sum_start(1)
-    give_back(2, lambda: sum_turn(1))
-    red = sum_end(1)
-    alpha2 = (red[0:1] / heading_image(red))[0, 0]
+    give_back(2)
+    sum_turn(1)
+
+    def close_step():
+        red = sum_end(1)
+        ratio = red[0:1] / heading_image(red)
+        last[...] = jnp.broadcast_to(ratio, (1, H))
+        a = ratio[0, 0]
+        for part in range(2):
+            step[part] = alpha_s * q0[part] + a * h2[part]
+
+    adjoint(2, resid, 1.0, close_step)
+    a = last[0:1, 0:1][0, 0]
     for part in range(2):
-        step[part] = alpha_s * q0[part] + alpha2 * h2[part]
-        resid[part] = q1[part] - alpha2 * resid[part]
-    adjoint(2, resid, -alpha2)
+        resid[part] = q1[part] - a * resid[part]
 
 
 def on_device(spectrum, measured, pupil_mask, led_count, led_owner, led_offset):
@@ -523,14 +570,14 @@
         return pltpu.VMEM(shape, F32)
 
     return pl.pallas_call(
-        kernel, out_shape=(out, out), in_specs=[VM] * 8, out_specs=(VM, VM),
+        kernel, out_shape=(out, out), in_specs=[VM, VM, VM, ANY, VM, VM, ANY, VM], out_specs=(VM, VM),
         scratch_shapes=[
-            vm(S, 2, B, B), vm(S, B, B), vm(2, S, B, H), vm(3, 2, 4, S + 2, 32, H), vm(3, 2, 4, S + 2, 32, H), vm(2, 2, N, 32, H),
-            vm(3, 2, 2, 4, N, 8, H), vm(3, 2, N, 32, H), vm(3, 2, N, 32, H), vm(2, 2, 3, S, 32, H), vm(3, S, 2, B, H),
-            vm(2, 2, N, 8, H), vm(3, 4, 2, T), vm(3, 4, 2, T), vm(2, T, T), vm(2, T, T), vm(2, T, T), vm(2, B, H),
+            vm(S, 2, B, B), vm(S, B, B), vm(2, S, B, H), vm(3, 2, 4, S + 2, 32, H), vm(3, 2, 4, S + 2, 32, H), vm(2, 2, 4, N, 8, H),
+            vm(3, 2, 2, 4, N, 8, H), vm(3, 2, 4, N, 8, H), vm(3, 2, 4, N, 8, H), vm(2, 3, S, 2, 32, H), vm(3, S, 2, B, H),
+            vm(2, 2, N, 8, H), vm(3, 4, 2, T), vm(3, 4, 2, T), vm(2, T, T), vm(2, T, T), vm(2, T, T), vm(2, B, H), vm(2, 2, B, B), vm(2, T, T), pltpu.VMEM((2, 4, B, B), BF), vm(1, H),
             pltpu.VMEM((40, H), jnp.int32), pltpu.SMEM((40, H), jnp.int32),
             vm(2, 8, H), vm(2, 16, 8, H), vm(2, 8, 8, H), vm(2, 8, H),
-            dma((3, 2, 12)), dma((3, S)), dma((2, 4)), dma(()),
+            dma((3, 2, 12)), dma((3, len(GROUPS))), dma((2, 4)), dma((3,)),
         ],
         compiler_params=pltpu.CompilerParams(collective_id=0, has_side_effects=True, vmem_limit_bytes=LIMIT),
         name="update",

time: 136 us -> 134 us (0.985)
  Pallas kernels: 133 us -> 130 us
    pallas_call x1, Pallas kernels: 133 us -> 130 us  [on_device(): pl.pallas_call(kernel, out_shape=(out, out), in_specs=[VM, VM, VM, ANY, V...]
where the time goes in v4:
time: 134 us; the launch traced here: 133 us
  Pallas kernels  130 us (97%)
  local copies, waits for them, and re-layouts  2.64 us (2%)
    pallas_call x1, Pallas kernels, on_device(): pl.pallas_call(kernel, out_shape=(out, out), in_specs=[VM, VM, VM, ANY, V...  130 us

profile of v4, /device:TPU:1, one launch (start us, length us, event | category | flops | bytes accessed | tf_op | source)
XLA Modules:
  0.0 133.3 jit_solution(5696269393872001150)
XLA Ops:
  0.6 130.0 %update.1 = (f32[2,512,512]{2,1,0:T(8,128)S(1)}, f32[2,512,512]{2,1,0:T(8,128)S(1)}) custom-call(s32[1,128]{1,0:T(1,128)} %bitcast.5, s32[8,128]{1,0:T(8,128)} %bitcast.4, s32[8,2,128]{2,1,0:T(2,128)} %bitcast.3, f32[2,512,512]{2,1,0:T(8,128)} %given.1, s32[256,256]{1,0:T(8,128)} %mask.1, f32[1,256,256]{2,1,0:T(8,128)} %measured.1, ...), custom_call_target="tpu_custom_call" | custom-call | tf_op jit(solution)/shard_map/update/pallas_call | solution.py:572
  130.6 1.3 copy.12
  131.9 1.3 copy.13

commit v5 on v4

--- a/solution.py
+++ b/solution.py
@@ -392,7 +392,7 @@
                 stage4(ph, q, *GROUPS[g])
             send4(ph, None, g)
 
-    def adjoint(ph, out, sign, late=None):
+    def adjoint(ph, out, sign, late=()):
         back[1] = jnp.zeros((2, B, B), F32)
 
         def add_in(s, which):
@@ -405,8 +405,8 @@
                 def _():
                     wait_got(wret.at[ph, low:high, :, 0:192, :], sem4.at[ph, g])
 
-            if late is not None:
-                pl.when(s == 5)(late)
+            for step_no, action in late:
+                pl.when(s == step_no)(action)
             odd = lax.rem(s, 2)
             add_in(jnp.maximum(s - 1, 0), 1 - odd)
             w = [wret[ph, s, q] * (2.0 * sign) for q in range(2)]
@@ -542,7 +542,6 @@
     ax[1, 1:2, :] = dot_rows(whole(h2), whole(resid))
     sum_start(1)
     give_back(2)
-    sum_turn(1)
 
     def close_step():
         red = sum_end(1)
@@ -552,7 +551,7 @@
         for part in range(2):
             step[part] = alpha_s * q0[part] + a * h2[part]
 
-    adjoint(2, resid, 1.0, close_step)
+    adjoint(2, resid, 1.0, ((2, lambda: sum_turn(1)), (6, close_step)))
     a = last[0:1, 0:1][0, 0]
     for part in range(2):
         resid[part] = q1[part] - a * resid[part]

time: 134 us -> 137 us (1.022)
  Pallas kernels: 130 us -> 133 us
    pallas_call x1, Pallas kernels: 130 us -> 133 us  [on_device(): pl.pallas_call(kernel, out_shape=(out, out), in_specs=[VM, VM, VM, ANY, V...]
where the time goes in v5:
time: 137 us
  Pallas kernels  133 us (97%)
  local copies, waits for them, and re-layouts  2.64 us (2%)
    pallas_call x1, Pallas kernels, on_device(): pl.pallas_call(kernel, out_shape=(out, out), in_specs=[VM, VM, VM, ANY, V...  133 us

profile of v5, /device:TPU:1, one launch (start us, length us, event | category | flops | bytes accessed | tf_op | source)
XLA Modules:
  0.0 136.7 jit_solution(13536000523742918309)
XLA Ops:
  0.6 133.4 %update.1 = (f32[2,512,512]{2,1,0:T(8,128)S(1)}, f32[2,512,512]{2,1,0:T(8,128)S(1)}) custom-call(s32[1,128]{1,0:T(1,128)} %bitcast.5, s32[8,128]{1,0:T(8,128)} %bitcast.4, s32[8,2,128]{2,1,0:T(2,128)} %bitcast.3, f32[2,512,512]{2,1,0:T(8,128)} %given.1, s32[256,256]{1,0:T(8,128)} %mask.1, f32[1,256,256]{2,1,0:T(8,128)} %measured.1, ...), custom_call_target="tpu_custom_call" | custom-call | tf_op jit(solution)/shard_map/update/pallas_call | solution.py:571
  134.1 1.3 copy.12
  135.4 1.3 copy.13
